TPU v7x, 32 devices: a whole 2x2x4 slice. The times are simulated.
32 devices in a mesh: dp: 4 (over z), seq: 4 (over x, core), mp: 2 (over y).
Axes of the slice: x: 2, y: 2, z: 4, core: 2. Of those that a mesh axis runs over, the one named last changes fastest.
Arguments:
- queries: bfloat16 [2048, 4096], P(('dp', 'seq'), 'mp'), may hold values from -2 to 2
- key_rows: bfloat16 [2048, 4096], P(('dp', 'seq'), 'mp'), may hold values from -2 to 2
- value_rows: bfloat16 [2048, 4096], P(('dp', 'seq'), 'mp'), may hold values from -6 to 6
- row_plan: int32 [4, 4], replicated, may hold values from 0 to 40, as said below
- segments: int32 [4, 512], P('dp', 'seq'), may hold values from 0 to 5, never falling along the last dimension, each value on 1 to 256 neighbouring positions
- norm_gain: float32 [4096], P('mp'), may hold values from 0.5 to 1.5
- out_weight: bfloat16 [4096, 3072], P('mp'), may hold values from -0.09375 to 0.09375
- out_grad: bfloat16 [2048, 3072], P(('dp', 'seq'), 'mp'), may hold values from -6 to 6
Outputs:
- normed: bfloat16 [2048, 4096], P(('dp', 'seq'), 'mp')
- query_grad: bfloat16 [2048, 4096], P(('dp', 'seq'), 'mp')
- key_grad: bfloat16 [2048, 4096], P(('dp', 'seq'), 'mp')
- value_grad: bfloat16 [2048, 4096], P(('dp', 'seq'), 'mp')
- weight_grad: float32 [3072, 4096], P(('dp', 'seq'), 'mp')
Inputs may be any that keep to these rules, and one draw needn't show every extreme that they name: Each row and each column of row_plan sums to 128; the plan holds for every sequence shard alike; an arriving group's rows for group 0 come first, then those for group 1, and so on. `segments`: documents never cross data groups.
All inputs are finite; a program needn't handle non-finite values.
Results may differ from a plain program's by a relative error of at most 0.0064.
Values may be sent and summed in bfloat16 or wider, within the bound.
A program may use at most 128 MiB of HBM per device.

v0:
```python
import functools

import jax
import jax.numpy as jnp
from jax import lax
from jax.experimental import pallas as pl
from jax.experimental.pallas import tpu as pltpu
from jax.sharding import PartitionSpec as P

HS = 128


NORM_EPS = 1e-06
F32 = jnp.float32
BF16 = jnp.bfloat16


def mm(a, b, ca, cb):
    return lax.dot_general(a, b, (((ca,), (cb,)), ((), ())), preferred_element_type=F32)


def place_body(blocks, pick_ref, tail_ref, aq_ref, ak_ref, av_ref, q_ref, k_ref, v_ref, st_ref):
    pick = pick_ref[...]
    tail = tail_ref[...]
    for src, dst in ((aq_ref, q_ref), (ak_ref, k_ref), (av_ref, v_ref)):
        dst[...] = mm(pick, src[...], 1, 0).astype(BF16)
    for h in range(blocks):
        cols = slice(h * HS, (h + 1) * HS)
        st_ref[:, cols] = mm(k_ref[:, cols] * tail, v_ref[:, cols], 0, 0)


def forward_body(
    blocks, doc_ref, carried_ref, headp_ref, gain_ref, q_ref, k_ref, v_ref, st_ref, dn_ref,
    normed_ref, dh_ref, r_ref,
):
    doc = doc_ref[...]
    carried = carried_ref[...]
    headp = headp_ref[...]
    for h in range(blocks):
        cols = slice(h * HS, (h + 1) * HS)
        q, k, v = q_ref[:, cols], k_ref[:, cols], v_ref[:, cols]
        p = (mm(q, k, 1, 1) * doc).astype(BF16)
        attn = mm(p, v, 1, 0) + mm(q, st_ref[:, cols], 1, 0) * carried
        gain = gain_ref[:, cols]
        scale = lax.rsqrt(jnp.mean(attn * attn, axis=-1, keepdims=True) + NORM_EPS)
        unit = attn * scale
        normed_ref[:, cols] = (unit * gain).astype(BF16)
        g = dn_ref[:, cols] * gain
        d_attn = scale * (g - unit * jnp.mean(g * unit, axis=-1, keepdims=True))
        d_half = d_attn.astype(BF16)
        dh_ref[:, cols] = d_half
        r_ref[:, cols] = mm(q * headp, d_half, 0, 0)


def backward_body(
    blocks, doc_ref, carried_ref, rev_ref, q_ref, k_ref, v_ref, d_ref, st_ref, rst_ref,
    dq_ref, dk_ref, dv_ref,
):
    doc = doc_ref[...]
    carried = carried_ref[...]
    rev = rev_ref[...]
    for h in range(blocks):
        cols = slice(h * HS, (h + 1) * HS)
        q, k, v, d = q_ref[:, cols], k_ref[:, cols], v_ref[:, cols], d_ref[:, cols]
        st, rst = st_ref[:, cols], rst_ref[:, cols]
        p = (mm(q, k, 1, 1) * doc).astype(BF16)
        dp = (mm(d, v, 1, 1) * doc).astype(BF16)
        dq_ref[:, cols] = (mm(dp, k, 1, 0) + mm(d, st, 1, 1) * carried).astype(BF16)
        dk_ref[:, cols] = (mm(dp, q, 0, 0) + mm(v, rst, 1, 1) * rev).astype(BF16)
        dv_ref[:, cols] = (mm(p, d, 0, 0) + mm(k, rst, 1, 0) * rev).astype(BF16)


def by_heads(body, heads, fixed, moving, outs):
    blocks = 4 if heads % 4 == 0 else 1
    span = blocks * HS
    rows_of = lambda a: pl.BlockSpec((a.shape[0], span), lambda i: (0, i))
    whole = lambda a: pl.BlockSpec(a.shape, lambda i: (0, 0))
    moved = sum(a.size * a.dtype.itemsize for a in (*fixed, *moving, *outs))
    return pl.pallas_call(
        functools.partial(body, blocks),
        grid=(heads // blocks,),
        in_specs=[whole(a) for a in fixed] + [rows_of(a) for a in moving],
        out_specs=[rows_of(a) for a in outs],
        out_shape=list(outs),
        cost_estimate=pl.CostEstimate(
            flops=16 * heads * HS * HS * HS, bytes_accessed=moved, transcendentals=0
        ),
    )(*fixed, *moving)


def chain(local, ids, axis, reverse):
    peers, place = lax.axis_size(axis), lax.axis_index(axis)
    step = -1 if reverse else 1
    before = jnp.take(ids, jnp.clip(place - step, 0, peers - 1))
    joined = before == jnp.take(ids, place)
    got = jnp.zeros(local.shape, BF16)
    for hop in range(peers - 1):
        at = peers - 1 - hop if reverse else hop
        sent = local if hop == 0 else local + jnp.where(joined, got.astype(F32), 0.0)
        got = got + lax.ppermute(sent.astype(BF16), axis, [(at, at + step)])
    first = place == (peers - 1 if reverse else 0)
    return got, jnp.where(first, jnp.full_like(before, -1.0), before)


def local(queries, key_rows, value_rows, row_plan, segments, norm_gain, out_weight, out_grad):
    row_total = queries.shape[0]
    width = queries.shape[1]
    heads = width // HS
    groups = lax.axis_size("dp")
    my_group = lax.axis_index("dp")
    devices = groups * lax.axis_size("seq")
    capacity = row_total // min(groups, 8) + row_total // 16
    slots_all = groups * capacity
    send_start = jnp.cumsum(row_plan, axis=1) - row_plan
    recv_start = jnp.cumsum(row_plan, axis=0) - row_plan
    slots = jnp.arange(capacity, dtype=jnp.int32)
    positions = jnp.arange(row_total, dtype=jnp.int32)
    my_send = jnp.take(send_start, my_group, axis=0)
    send_index = jnp.minimum(my_send[:, None] + slots[None, :], row_total - 1).reshape(-1)
    send_hot = (send_index[:, None] == positions[None, :]).astype(BF16)

    def hand(x):
        packed = jnp.dot(send_hot, x, preferred_element_type=F32).astype(BF16)
        return lax.all_to_all(packed, "dp", split_axis=0, concat_axis=0, tiled=True)

    arrived = (hand(queries), hand(key_rows), hand(value_rows))
    my_start = jnp.take(recv_start, my_group, axis=1)
    my_end = my_start + jnp.take(row_plan, my_group, axis=1)
    source = jnp.sum((my_end[None, :] <= positions[:, None]).astype(jnp.int32), axis=1)
    pick = source * capacity + positions - jnp.take(my_start, source)
    pick_hot = (pick[:, None] == jnp.arange(slots_all, dtype=jnp.int32)[None, :]).astype(BF16)

    seg_f = segments[0].astype(F32)
    edges = lax.all_gather(jnp.stack([seg_f[0], seg_f[-1]]), "seq")
    causal = positions[None, :] <= positions[:, None]
    same_doc = (causal & (seg_f[:, None] == seg_f[None, :])).astype(F32)
    tail = (seg_f == seg_f[-1]).astype(BF16)[:, None]
    head_part = (seg_f == seg_f[0]).astype(BF16)[:, None]

    full_grad = lax.all_gather(out_grad, "mp", axis=1, tiled=True)
    d_normed = lax.dot_general(
        full_grad, out_weight, (((1,), (1,)), ((), ())), preferred_element_type=F32
    )
    grad_cols = full_grad.T.reshape(devices, full_grad.shape[1] // devices, row_total)
    grad_cols = lax.all_to_all(grad_cols, ("dp", "seq"), split_axis=0, concat_axis=0, tiled=True)

    half = jax.ShapeDtypeStruct((row_total, width), BF16)
    state = jax.ShapeDtypeStruct((HS, width), F32)
    q, k, v, local_state = by_heads(
        place_body, heads, (pick_hot, tail), arrived, (half, half, half, state)
    )
    state_in, id_in = chain(local_state, edges[:, 1], "seq", False)
    carried = (seg_f == id_in).astype(F32)[:, None]
    gain_row = norm_gain.reshape(1, width)
    normed, d_half, local_r = by_heads(
        forward_body,
        heads,
        (same_doc, carried, head_part),
        (gain_row, q, k, v, state_in, d_normed),
        (half, half, state),
    )
    everyone = lax.all_gather(normed, ("dp", "seq"), axis=0)
    rstate_in, rid_in = chain(local_r, edges[:, 0], "seq", True)
    rev_use = (seg_f == rid_in).astype(F32)[:, None]
    dquery, dkey, dvalue = by_heads(
        backward_body,
        heads,
        (same_doc, carried, rev_use),
        (q, k, v, d_half, state_in, rstate_in),
        (half, half, half),
    )
    weight_grad = lax.dot_general(
        grad_cols, everyone, (((0, 2), (0, 1)), ((), ())), preferred_element_type=F32
    )
    return normed, dquery, dkey, dvalue, weight_grad


def solution(mesh):
    placed = (
        P(("dp", "seq"), "mp"),
        P(("dp", "seq"), "mp"),
        P(("dp", "seq"), "mp"),
        P(),
        P("dp", "seq"),
        P("mp"),
        P("mp", None),
        P(("dp", "seq"), "mp"),
    )
    return jax.shard_map(
        local,
        mesh=mesh,
        in_specs=placed,
        out_specs=(
            P(("dp", "seq"), "mp"),
            P(("dp", "seq"), "mp"),
            P(("dp", "seq"), "mp"),
            P(("dp", "seq"), "mp"),
            P(("dp", "seq"), "mp"),
        ),
        check_vma=False,
    )
```

profile of v0, /device:TPU:0, one launch (start us, length us, event | category | flops | bytes accessed | tf_op | source)
XLA Modules:
  0.0 221.9 jit_solution(12133292273872337727)
XLA Ops:
  10.9 6.3 %all-to-all-start = ((bf16[4,40,2048]{2,1,0:T(8,128)(2,1)}), bf16[4,40,2048]{2,1,0:T(8,128)(2,1)S(1)}, u32[]{:S(2)}, u32[]{:S(2)}) async-start(bf16[4,40,2048]{2,1,0:T(8,128)(2,1)} %bitcast.20), calls=%async_computation | async-start | bytes 1310720 | tf_op jit(solution)/shard_map/all_to_all | solution.py:124
  17.3 2.3 %convolution_convert_fusion.1 = bf16[160,2048]{1,0:T(8,128)(2,1)} fusion(bf16[128,2048]{1,0:T(8,128)(2,1)} %param.11, s32[160]{0:T(256)S(1)} %min.23), kind=kOutput, calls=%fused_computation.2 | convolution fusion | flops 84234240 | bytes 1180288 | tf_op jit(solution)/shard_map/dot_general | solution.py:123
  19.5 15.0 %all-to-all-done = bf16[4,40,2048]{2,1,0:T(8,128)(2,1)S(1)} async-done(((bf16[4,40,2048]{2,1,0:T(8,128)(2,1)}), bf16[4,40,2048]{2,1,0:T(8,128)(2,1)S(1)}, u32[]{:S(2)}, u32[]{:S(2)}) %all-to-all-start) | async-done | bytes 655392 | tf_op jit(solution)/shard_map/all_to_all | solution.py:124
  34.6 3.5 %all-to-all-start.1 = ((bf16[4,40,2048]{2,1,0:T(8,128)(2,1)}), bf16[4,40,2048]{2,1,0:T(8,128)(2,1)S(1)}, u32[]{:S(2)}, u32[]{:S(2)}) async-start(bf16[4,40,2048]{2,1,0:T(8,128)(2,1)} %bitcast.22), calls=%async_computation.1 | async-start | bytes 1310720 | tf_op jit(solution)/shard_map/all_to_all | solution.py:124
  42.7 6.1 %all-reduce = f32[8]{0:T(128)S(1)} all-reduce(f32[8]{0:T(128)S(1)} %maximum_dynamic-update-slice_fusion), channel_id=2, replica_groups=mesh['dp'=4,'seq'=4,'mp'=2] {'seq'}, use_global_device_ids=true, to_apply=%add | all-reduce | flops 8 | bytes 64
  48.9 2.2 %convolution_convert_fusion = bf16[160,2048]{1,0:T(8,128)(2,1)} fusion(bf16[128,2048]{1,0:T(8,128)(2,1)} %param.12, s32[160]{0:T(256)S(1)} %min.23), kind=kOutput, calls=%fused_computation.1 | convolution fusion | flops 84234240 | bytes 1180288 | tf_op jit(solution)/shard_map/dot_general | solution.py:123
  51.1 3.8 %all-to-all-done.1 = bf16[4,40,2048]{2,1,0:T(8,128)(2,1)S(1)} async-done(((bf16[4,40,2048]{2,1,0:T(8,128)(2,1)}), bf16[4,40,2048]{2,1,0:T(8,128)(2,1)S(1)}, u32[]{:S(2)}, u32[]{:S(2)}) %all-to-all-start.1) | async-done | bytes 655392 | tf_op jit(solution)/shard_map/all_to_all | solution.py:124
  54.9 3.5 %all-to-all-start.2 = ((bf16[4,40,2048]{2,1,0:T(8,128)(2,1)}), bf16[4,40,2048]{2,1,0:T(8,128)(2,1)S(1)}, u32[]{:S(2)}, u32[]{:S(2)}) async-start(bf16[4,40,2048]{2,1,0:T(8,128)(2,1)} %bitcast.24), calls=%async_computation.2 | async-start | bytes 1310720 | tf_op jit(solution)/shard_map/all_to_all | solution.py:124
  60.3 2.0 fusion.11
  64.6 2.5 %fusion.9 = s32[128]{0:T(128)S(1)} fusion(s32[128]{0:T(128)S(1)} %convert_reduce_fusion, s32[]{:T(128)} %bitcast.12, s32[]{:T(128)} %bitcast.13, s32[]{:T(128)} %bitcast.15, s32[]{:T(128)} %bitcast.14), kind=kLoop, calls=%fused_computation.41 | loop fusion | flops 2432 | bytes 1040 | tf_op jit(solution)/shard_map/sub | solution.py:130
  67.8 7.4 %all-to-all-done.2 = bf16[4,40,2048]{2,1,0:T(8,128)(2,1)S(1)} async-done(((bf16[4,40,2048]{2,1,0:T(8,128)(2,1)}), bf16[4,40,2048]{2,1,0:T(8,128)(2,1)S(1)}, u32[]{:S(2)}, u32[]{:S(2)}) %all-to-all-start.2) | async-done | bytes 655392 | tf_op jit(solution)/shard_map/all_to_all | solution.py:124
  76.0 4.6 %shard_map.119 = (bf16[128,2048]{1,0:T(8,128)(2,1)}, bf16[128,2048]{1,0:T(8,128)(2,1)}, bf16[128,2048]{1,0:T(8,128)(2,1)}, f32[128,2048]{1,0:T(8,128)}) custom-call(bf16[128,160]{1,0:T(8,128)(2,1)} %fusion.pick_ref, bf16[128,1]{1,0:T(8,128)(2,1)} %copy.25.tail_ref, bf16[160,2048]{1,0:T(8,128)(2,1)} %bitcast.60, bf16[160,2048]{1,0:T(8,128)(2,1)} %bitcast.61, ...), custom_call_target="tpu_custom_call" | custom-call | flops 536870912 | bytes 4628736 | tf_op jit(solution)/shard_map/pallas_call | solution.py:79
  88.2 12.2 %all_gather.17 = bf16[128,3072]{1,0:T(8,128)(2,1)S(1)} all-gather(bf16[128,1536]{1,0:T(8,128)(2,1)S(1)} %copy-done.4), channel_id=1, replica_groups=mesh['dp'=4,'seq'=4,'mp'=2] {'mp'}, dimensions={1}, use_global_device_ids=true | all-gather | bytes 1179648 | tf_op jit(solution)/shard_map/all_gather | solution.py:140
  101.2 1.5 add_convert_fusion.2
  103.4 9.8 %fusion.18.dn_ref = f32[128,2048]{1,0:T(8,128)} fusion(bf16[128,3072]{1,0:T(8,128)(2,1)S(1)} %all_gather.17, bf16[2048,3072]{1,0:T(8,128)(2,1)} %param.16), kind=kOutput, calls=%fused_computation.52 | convolution fusion | flops 1610612736 | bytes 14417920 | tf_op jit(solution)/shard_map/dot_general | solution.py:141
  114.1 8.8 %shard_map.120 = (bf16[128,2048]{1,0:T(8,128)(2,1)}, bf16[128,2048]{1,0:T(8,128)(2,1)}, f32[128,2048]{1,0:T(8,128)}) custom-call(f32[128,128]{1,0:T(8,128)} %fusion.2.doc_ref, f32[128,1]{1,0:T(8,128)} %copy.26.carried_ref, bf16[128,1]{1,0:T(8,128)(2,1)} %copy.27.headp_ref, f32[1,2048]{1,0:T(1,128)} %bitcast.63, bf16[128,2048]{1,0:T(8,128)(2,1)} %get-tuple-element.16.q_ref, ...), custom_call_target="tpu_custom_call" | custom-call | flops 536870912 | bytes 5317376 | tf_op jit(solution)/shard_map/pallas_call | solution.py:79
  126.8 1.5 collective-permute-start.4
  129.5 5.4 %all-to-all-start.3 = ((bf16[16,192,128]{2,1,0:T(8,128)(2,1)}), bf16[16,192,128]{2,1,0:T(8,128)(2,1)S(1)}, u32[]{:S(2)}, u32[]{:S(2)}) async-start(bf16[16,192,128]{2,1,0:T(8,128)(2,1)} %bitcast.37), calls=%async_computation.3 | async-start | bytes 1572864 | tf_op jit(solution)/shard_map/all_to_all | solution.py:145
  134.8 1.6 add_convert_fusion
  138.5 12.2 %collective-permute-done.5 = bf16[128,2048]{1,0:T(8,128)(2,1)S(1)} collective-permute-done((bf16[128,2048]{1,0:T(8,128)(2,1)S(1)}, bf16[128,2048]{1,0:T(8,128)(2,1)S(1)}, u32[]{:S(2)}, u32[]{:S(2)}) %collective-permute-start.5) | collective-permute-done | bytes 524320 | tf_op jit(solution)/shard_map/ppermute | solution.py:100
  151.7 6.5 %shard_map.121 = (bf16[128,2048]{1,0:T(8,128)(2,1)}, bf16[128,2048]{1,0:T(8,128)(2,1)}, bf16[128,2048]{1,0:T(8,128)(2,1)}) custom-call(f32[128,128]{1,0:T(8,128)} %fusion.2.doc_ref, f32[128,1]{1,0:T(8,128)} %copy.26.carried_ref, f32[128,1]{1,0:T(8,128)} %copy.29.rev_ref, bf16[128,2048]{1,0:T(8,128)(2,1)} %get-tuple-element.16.q_ref, ...), custom_call_target="tpu_custom_call" | custom-call | flops 536870912 | bytes 4785152 | tf_op jit(solution)/shard_map/pallas_call | solution.py:79
  158.1 6.5 %all-to-all-done.3 = bf16[16,192,128]{2,1,0:T(8,128)(2,1)S(1)} async-done(((bf16[16,192,128]{2,1,0:T(8,128)(2,1)}), bf16[16,192,128]{2,1,0:T(8,128)(2,1)S(1)}, u32[]{:S(2)}, u32[]{:S(2)}) %all-to-all-start.3) | async-done | bytes 786464 | tf_op jit(solution)/shard_map/all_to_all | solution.py:145
  164.6 44.8 %all-gather.4.cloned.1.call-done = bf16[2048,2048]{1,0:T(8,128)(2,1)} async-done(((bf16[128,2048]{1,0:T(8,128)(2,1)}), bf16[2048,2048]{1,0:T(8,128)(2,1)}) %all-gather.4.cloned.1.call-update) | async-done | bytes 8388624 | tf_op jit(solution)/shard_map/all_gather | solution.py:162
  209.4 5.7 %convolution_bitcast_fusion = f32[192,2048]{1,0:T(8,128)} fusion(bf16[16,192,128]{2,1,0:T(8,128)(2,1)S(1)} %all-to-all-done.3, bf16[16,128,2048]{2,1,0:T(8,128)(2,1)} %bitcast.64), kind=kOutput, calls=%fused_computation | convolution fusion | flops 1610612736 | bytes 10747904 | tf_op jit(solution)/shard_map/dot_general | solution.py:172
  (54 shorter events, 29.2 us)
Async XLA Ops:
  7.2 2.5 %copy-start = (bf16[128,2048]{1,0:T(8,128)(2,1)S(1)}, bf16[128,2048]{1,0:T(8,128)(2,1)}, u32[]{:S(2)}) copy-start(bf16[128,2048]{1,0:T(8,128)(2,1)} %param.10) | copy-start | bytes 1572868
  7.2 81.1 %copy-start.4 = (bf16[128,1536]{1,0:T(8,128)(2,1)S(1)}, bf16[128,1536]{1,0:T(8,128)(2,1)}, u32[]{:S(2)}) copy-start(bf16[128,1536]{1,0:T(8,128)(2,1)} %param.17) | copy-start | bytes 1179652
  10.9 23.6 %all-to-all-start = ((bf16[4,40,2048]{2,1,0:T(8,128)(2,1)}), bf16[4,40,2048]{2,1,0:T(8,128)(2,1)S(1)}, u32[]{:S(2)}, u32[]{:S(2)}) async-start(bf16[4,40,2048]{2,1,0:T(8,128)(2,1)} %bitcast.20), calls=%async_computation | async-start | bytes 1310720 | tf_op jit(solution)/shard_map/all_to_all | solution.py:124
  34.6 40.6 %copy-start.1 = (bf16[4,40,2048]{2,1,0:T(8,128)(2,1)}, bf16[4,40,2048]{2,1,0:T(8,128)(2,1)S(1)}, u32[]{:S(2)}) copy-start(bf16[4,40,2048]{2,1,0:T(8,128)(2,1)S(1)} %all-to-all-done) | copy-start | bytes 1966084
  34.6 20.3 %all-to-all-start.1 = ((bf16[4,40,2048]{2,1,0:T(8,128)(2,1)}), bf16[4,40,2048]{2,1,0:T(8,128)(2,1)S(1)}, u32[]{:S(2)}, u32[]{:S(2)}) async-start(bf16[4,40,2048]{2,1,0:T(8,128)(2,1)} %bitcast.22), calls=%async_computation.1 | async-start | bytes 1310720 | tf_op jit(solution)/shard_map/all_to_all | solution.py:124
  54.9 20.3 %copy-start.2 = (bf16[4,40,2048]{2,1,0:T(8,128)(2,1)}, bf16[4,40,2048]{2,1,0:T(8,128)(2,1)S(1)}, u32[]{:S(2)}) copy-start(bf16[4,40,2048]{2,1,0:T(8,128)(2,1)S(1)} %all-to-all-done.1) | copy-start | bytes 1966084
  54.9 20.3 %all-to-all-start.2 = ((bf16[4,40,2048]{2,1,0:T(8,128)(2,1)}), bf16[4,40,2048]{2,1,0:T(8,128)(2,1)S(1)}, u32[]{:S(2)}, u32[]{:S(2)}) async-start(bf16[4,40,2048]{2,1,0:T(8,128)(2,1)} %bitcast.24), calls=%async_computation.2 | async-start | bytes 1310720 | tf_op jit(solution)/shard_map/all_to_all | solution.py:124
  58.4 151.0 %all-gather.4.cloned.1.call-start = ((), (), s32[]{:S(2)}) async-start(), calls=%async_computation.4 | async-start | bytes 8912896 | tf_op jit(solution)/shard_map/all_gather | solution.py:162
  75.2 0.8 copy-start.3
  81.9 2.8 %collective-permute-start = (bf16[128,2048]{1,0:T(8,128)(2,1)S(1)}, bf16[128,2048]{1,0:T(8,128)(2,1)S(1)}, u32[]{:S(2)}, u32[]{:S(2)}) collective-permute-start(bf16[128,2048]{1,0:T(8,128)(2,1)S(1)} %convert_element_type.145), channel_id=1, source_target_pairs={{0,2},{1,3},{8,10},{9,11},{16,18},{17,19},{24,26},{25,27}} | collective-permute-start | bytes 1572872 | tf_op jit(solution)/shard_map/ppermute | solution.py:100
  86.1 15.1 %collective-permute-start.1 = (bf16[128,2048]{1,0:T(8,128)(2,1)S(1)}, bf16[128,2048]{1,0:T(8,128)(2,1)S(1)}, u32[]{:S(2)}, u32[]{:S(2)}) collective-permute-start(bf16[128,2048]{1,0:T(8,128)(2,1)S(1)} %add_convert_fusion.3), channel_id=1, source_target_pairs={{2,4},{3,5},{10,12},{11,13},{18,20},{19,21},{26,28},{27,29}} | collective-permute-start | bytes 1572872 | tf_op jit(solution)/shard_map/ppermute | solution.py:100
  102.7 10.5 %collective-permute-start.2 = (bf16[128,2048]{1,0:T(8,128)(2,1)S(1)}, bf16[128,2048]{1,0:T(8,128)(2,1)S(1)}, u32[]{:S(2)}, u32[]{:S(2)}) collective-permute-start(bf16[128,2048]{1,0:T(8,128)(2,1)S(1)} %get-tuple-element.94), channel_id=1, source_target_pairs={{4,6},{5,7},{12,14},{13,15},{20,22},{21,23},{28,30},{29,31}} | collective-permute-start | bytes 1572872 | tf_op jit(solution)/shard_map/ppermute | solution.py:100
  124.2 1.3 collective-permute-start.3
  126.8 8.0 %collective-permute-start.4 = (bf16[128,2048]{1,0:T(8,128)(2,1)S(1)}, bf16[128,2048]{1,0:T(8,128)(2,1)}, u32[]{:S(2)}, u32[]{:S(2)}) collective-permute-start(bf16[128,2048]{1,0:T(8,128)(2,1)S(1)} %add_convert_fusion.1), channel_id=1, source_target_pairs={{4,2},{5,3},{12,10},{13,11},{20,18},{21,19},{28,26},{29,27}} | collective-permute-start | bytes 1572872 | tf_op jit(solution)/shard_map/ppermute | solution.py:100
  129.5 35.2 %all-to-all-start.3 = ((bf16[16,192,128]{2,1,0:T(8,128)(2,1)}), bf16[16,192,128]{2,1,0:T(8,128)(2,1)S(1)}, u32[]{:S(2)}, u32[]{:S(2)}) async-start(bf16[16,192,128]{2,1,0:T(8,128)(2,1)} %bitcast.37), calls=%async_computation.3 | async-start | bytes 1572864 | tf_op jit(solution)/shard_map/all_to_all | solution.py:145
  136.5 14.2 %collective-permute-start.5 = (bf16[128,2048]{1,0:T(8,128)(2,1)S(1)}, bf16[128,2048]{1,0:T(8,128)(2,1)S(1)}, u32[]{:S(2)}, u32[]{:S(2)}) collective-permute-start(bf16[128,2048]{1,0:T(8,128)(2,1)S(1)} %get-tuple-element.92), channel_id=1, source_target_pairs={{2,0},{3,1},{10,8},{11,9},{18,16},{19,17},{26,24},{27,25}} | collective-permute-start | bytes 1572872 | tf_op jit(solution)/shard_map/ppermute | solution.py:100
Sparse Core Ops, SparseCore 0:
  123.0 86.3 all-gather.3
where the time goes:
time: 223 us; the launch traced here: 222 us
  waiting for transfers between devices  90.5 us (41%)
  starting transfers between devices  24.9 us (11%)
  other arithmetic  21.7 us (10%)
  matrix products  21.2 us (10%)
  Pallas kernels  19.8 us (9%)
  blocking collectives  18.4 us (8%)
  between operations  17.3 us (8%)
  local copies, waits for them, and re-layouts  8.19 us (4%)
    all_gather x1, waiting for transfers between devices, local(): everyone = lax.all_gather(normed, ('dp', 'seq'), axis=0)  44.8 us
    all_to_all x3, waiting for transfers between devices, hand(): return lax.all_to_all(packed, 'dp', split_axis=0, concat_axis=0, tiled=True)  26.2 us
    pallas_call x3, Pallas kernels, by_heads(): pl.pallas_call(functools.partial(body, blocks), grid=(heads // blocks,),...  19.8 us
    all_to_all x3, starting transfers between devices, hand(): return lax.all_to_all(packed, 'dp', split_axis=0, concat_axis=0, tiled=True)  13.3 us
    ppermute x6, waiting for transfers between devices, chain(): got = got + lax.ppermute(sent.astype(BF16), axis, [(at, at + step)])  13.1 us
    all_gather x1, blocking collectives, local(): full_grad = lax.all_gather(out_grad, 'mp', axis=1, tiled=True)  12.2 us
    dot_general x1, matrix products, local(): lax.dot_general(full_grad, out_weight, (((1,), (1,)), ((), ())), preferre...  9.8 us
    convert_element_type x6, other arithmetic, chain(): got = got + lax.ppermute(sent.astype(BF16), axis, [(at, at + step)])  8.4 us
  transfers between devices with their start and end apart: 11, of which 7 were waited for; matrix products, arithmetic and copies ran while one was open for 16% of the time, Pallas kernels for 3%

commit v1 on v0

v1 whole, which is shorter than its diff:
```python
import functools

import jax
import jax.numpy as jnp
from jax import lax
from jax.experimental import pallas as pl
from jax.experimental.pallas import tpu as pltpu
from jax.sharding import PartitionSpec as P

HS = 128
NORM_EPS = 1e-06
F32 = jnp.float32
BF16 = jnp.bfloat16
MESH = pl.DeviceIdType.MESH
K, V, Q = 0, 1, 2


def mm(a, b, ca, cb):
    return lax.dot_general(a, b, (((ca,), (cb,)), ((), ())), preferred_element_type=F32)


def plan_sizes(mesh, rows, width, out_half):
    groups, shards, splits = mesh.shape["dp"], mesh.shape["seq"], mesh.shape["mp"]
    z = {}
    z["D"], z["S"], z["M"], z["X"] = groups, shards, splits, shards // 2
    z["R"], z["W"], z["DM"] = rows, width, out_half
    z["DOUT"] = out_half * splits
    heads = width // HS
    z["HC"] = 4 if heads % 4 == 0 else 1
    z["NC"] = heads // z["HC"]
    z["CW"] = z["HC"] * HS
    z["CAP"] = rows // min(groups, 8) + rows // 16
    z["CP"] = -(-z["CAP"] // 16) * 16
    z["RB"] = z["DOUT"] // (groups * shards)
    z["PX"] = splits // z["X"]
    z["RP"] = z["RB"] // z["PX"]
    return z


def scratch_of(z):
    D, M, X, R, W, NC, CW = (z[n] for n in ("D", "M", "X", "R", "W", "NC", "CW"))
    XO = max(1, X - 1)
    vm = pltpu.VMEM
    dma = pltpu.SemaphoreType.DMA
    return dict(
        x=vm((3, R, W), BF16),
        snd=vm((3, NC, D, z["CP"], CW), BF16),
        arr=vm((3, NC, D, z["CP"], CW), BF16),
        f=vm((3, NC, R, CW), BF16),
        w=vm((NC, CW, z["DOUT"]), BF16),
        g=vm((M, R, z["DM"]), BF16),
        gt=vm((z["DOUT"], R), BF16),
        gz=vm((D, 2, X, z["RB"], R), BF16),
        lhs=vm((X, z["RB"], D * 2 * R), BF16),
        dn=vm((NC, R, CW), F32),
        pm=vm((NC, R, CW), BF16),
        lf=vm((HS, CW), F32),
        ls=vm((NC, HS, CW), BF16),
        st=vm((NC, HS, CW), BF16),
        rf=vm((NC, HS, CW), F32),
        lr=vm((NC, HS, CW), BF16),
        rst=vm((NC, HS, CW), BF16),
        dh=vm((NC, R, CW), BF16),
        nb=vm((NC, D, 2, R, CW), BF16),
        do=vm((3, NC, R, CW), BF16),
        acc=vm((NC, z["RB"], CW), F32),
        xs=vm((NC, XO, z["RB"], CW), BF16),
        xr=vm((NC, XO, z["RB"], CW), BF16),
        seg=vm((3, 8, R), F32),
        doc=vm((R, R), F32),
        mk=vm((4, R, R), BF16),
        jn=vm((2, 8, R), F32),
        sel=vm((D * z["CP"], R), BF16),
        pick=vm((R, D * z["CP"]), BF16),
        in_s=dma((4,)),
        w_s=dma((NC,)),
        y_ss=dma((max(1, M - 1),)),
        y_rs=dma((max(1, M - 1),)),
        sg_ss=dma((2,)),
        sg_rs=dma((2,)),
        r_ss=dma((3, NC, D)),
        r_rs=dma((3, NC, D)),
        g_ss=dma((2 * D,)),
        g_rs=dma((2 * D,)),
        b_ss=dma((max(1, M - 1),)),
        b_rs=dma((max(1, M - 1),)),
        f_ss=dma((NC,)),
        f_rs=dma((NC,)),
        v_ss=dma((NC,)),
        v_rs=dma((NC,)),
        nr_ss=dma((NC, D)),
        nl_ss=dma((NC, D)),
        n_rs=dma((NC, D)),
        p_ss=dma((NC, D)),
        p_rs=dma((NC, D)),
        x_ss=dma((NC, XO)),
        x_rs=dma((NC, XO)),
        o_s=dma((5, NC)),
    )


TAIL, HEAD, CAR, REV = 0, 1, 2, 3


def whole_body(z, names, *refs):
    plan, seg_in, gain, q_in, k_in, v_in, w_in, g_in = refs[:8]
    normed_out, dq_out, dk_out, dv_out, wg_out = refs[8:13]
    b = dict(zip(names, refs[13:]))
    D, S, M, X, R, NC, CW, HC = (z[n] for n in ("D", "S", "M", "X", "R", "NC", "CW", "HC"))
    CAP, CP, RB, RP, PX, DM = (z[n] for n in ("CAP", "CP", "RB", "RP", "PX", "DM"))
    d, s, m = lax.axis_index("dp"), lax.axis_index("seq"), lax.axis_index("mp")
    xi, co = s // 2, s % 2
    sent = []

    def remote(src, dst, ss, rs, **where):
        return pltpu.make_async_remote_copy(
            src_ref=src, dst_ref=dst, send_sem=ss, recv_sem=rs, device_id=where, device_id_type=MESH
        )

    def when(cond, act):
        if cond is None:
            act()
        else:
            pl.when(cond)(act)

    def go(copy, cond=None):
        when(cond, copy.start)
        sent.append((cond, copy))

    sources = ((k_in, b["x"].at[K]), (v_in, b["x"].at[V]), (q_in, b["x"].at[Q]), (g_in, b["g"].at[m]))
    loads = [pltpu.make_async_copy(a, c, b["in_s"].at[i]) for i, (a, c) in enumerate(sources)]
    for i in (0, 3, 1, 2):
        loads[i].start()
    w_loads = [
        pltpu.make_async_copy(w_in.at[pl.ds(c * CW, CW), :], b["w"].at[c], b["w_s"].at[c])
        for c in range(NC)
    ]

    own_seg = seg_in[...].astype(F32)
    b["seg"][0] = jnp.broadcast_to(own_seg, (8, R))
    if CP > CAP:
        b["arr"][:, :, :, CAP:CP, :] = jnp.zeros((3, NC, D, CP - CAP, CW), BF16)

    @pl.when(s == 0)
    def _():
        b["seg"][1] = jnp.full((8, R), -1.0, F32)
        b["st"][...] = jnp.zeros_like(b["st"])

    @pl.when(s == S - 1)
    def _():
        b["seg"][2] = jnp.full((8, R), -1.0, F32)
        b["rst"][...] = jnp.zeros_like(b["rst"])

    barrier = pltpu.get_barrier_semaphore()
    peers = 0

    def greet(**where):
        pl.semaphore_signal(barrier, inc=1, device_id=where, device_id_type=MESH)

    for t in range(D):
        for cc in range(2):
            if t or cc:
                greet(dp=lax.rem(d + t, D), seq=xi * 2 + (co + cc) % 2, mp=m)
                peers += 1
    for t in range(1, X):
        for cc in range(2):
            greet(dp=d, seq=lax.rem(xi + t, X) * 2 + cc, mp=m)
            peers += 1
    for t in range(1, M):
        greet(dp=d, seq=s, mp=lax.rem(m + t, M))
        peers += 1

    slot = lax.broadcasted_iota(jnp.int32, (D * CP, R), 0)
    row = lax.broadcasted_iota(jnp.int32, (D * CP, R), 1)
    start = jnp.int32(0)
    hot = jnp.zeros((D * CP, R), F32)
    for j in range(D):
        inside = (slot >= j * CP) & (slot < j * CP + CAP) & (row - start == slot - j * CP)
        hot = jnp.where(inside, 1.0, hot)
        start = start + plan[d, j]
    b["sel"][...] = hot.astype(BF16)
    slot = lax.broadcasted_iota(jnp.int32, (R, D * CP), 1)
    row = lax.broadcasted_iota(jnp.int32, (R, D * CP), 0)
    start = jnp.int32(0)
    hot = jnp.zeros((R, D * CP), F32)
    for i in range(D):
        count = plan[i, d]
        at = slot - i * CP
        inside = (at >= 0) & (at < CP) & (at == row - start) & (row - start < count)
        hot = jnp.where(inside, 1.0, hot)
        start = start + count
    b["pick"][...] = hot.astype(BF16)

    pl.semaphore_wait(barrier, peers)

    loads[3].wait()
    y_copies = []
    for t in range(1, M):
        c = remote(
            b["g"].at[m], b["g"].at[m], b["y_ss"].at[t - 1], b["y_rs"].at[t - 1], mp=lax.rem(m + t, M)
        )
        go(c)
        y_copies.append(c)
    after = remote(b["seg"].at[0], b["seg"].at[1], b["sg_ss"].at[0], b["sg_rs"].at[0], seq=lax.rem(s + 1, S))
    before = remote(
        b["seg"].at[0], b["seg"].at[2], b["sg_ss"].at[1], b["sg_rs"].at[1], seq=lax.rem(s + S - 1, S)
    )
    go(after, s < S - 1)
    go(before, s > 0)

    r_copies = {}

    def hand(a, c):
        packed = mm(b["sel"][...], b["x"][a, :, c * CW : (c + 1) * CW], 1, 0).astype(BF16)
        b["snd"][a, c] = packed.reshape(D, CP, CW)
        for t in range(1, D):
            to = lax.rem(d + t, D)
            copy = remote(
                b["snd"].at[a, c, to, pl.ds(0, CAP)],
                b["arr"].at[a, c, d, pl.ds(0, CAP)],
                b["r_ss"].at[a, c, t],
                b["r_rs"].at[a, c, t],
                dp=to,
            )
            go(copy)
            r_copies[a, c, t] = copy
        b["arr"][a, c, d] = b["snd"][a, c, d]

    loads[0].wait()
    loads[1].wait()
    for c in range(NC):
        hand(K, c)
        hand(V, c)
    for c in range(NC):
        w_loads[c].start()
    loads[2].wait()
    for c in range(NC):
        hand(Q, c)

    pl.when(s > 0)(after.wait_recv)
    pl.when(s < S - 1)(before.wait_recv)
    across = jnp.broadcast_to(b["seg"][0][0:1, :], (R, R))
    down = jnp.transpose(across)
    t_at = lax.broadcasted_iota(jnp.int32, (R, R), 0)
    u_at = lax.broadcasted_iota(jnp.int32, (R, R), 1)
    b["doc"][...] = jnp.where((u_at <= t_at) & (across == down), 1.0, 0.0)
    own_last = b["seg"][0][0:1, R - 1 : R]
    own_first = b["seg"][0][0:1, 0:1]
    last_before = b["seg"][1][0:1, R - 1 : R]
    first_after = b["seg"][2][0:1, 0:1]
    for i, value in ((TAIL, own_last), (HEAD, own_first), (CAR, last_before), (REV, first_after)):
        b["mk"][i] = jnp.where(down == jnp.broadcast_to(value, (R, R)), 1.0, 0.0).astype(BF16)
    for i, (one, two) in enumerate(((own_last, last_before), (own_first, first_after))):
        b["jn"][i] = jnp.broadcast_to(jnp.where(one == two, 1.0, 0.0), (8, R))

    for c in y_copies:
        c.wait_recv()
    for i in range(M):
        for j in range(DM // HS):
            b["gt"][pl.ds(i * DM + j * HS, HS), :] = jnp.transpose(b["g"][i, :, j * HS : (j + 1) * HS])
    px, off = m // PX, pl.multiple_of((m % PX) * RP, RP)
    g_copies = []
    for t in range(D):
        for cc in range(2):
            to, core = lax.rem(d + t, D), (co + cc) % 2
            at = pl.multiple_of(((to * X + px) * 2 + core) * RB + off, RP)
            if t == 0 and cc == 0:
                b["gz"][d, co, px, pl.ds(off, RP), :] = b["gt"][pl.ds(at, RP), :]
                continue
            copy = remote(
                b["gt"].at[pl.ds(at, RP), :],
                b["gz"].at[d, co, px, pl.ds(off, RP), :],
                b["g_ss"].at[t * 2 + cc],
                b["g_rs"].at[t * 2 + cc],
                dp=to,
                seq=xi * 2 + core,
            )
            go(copy)
            g_copies.append(copy)

    for c in range(NC):
        w_loads[c].wait()

    def grow(c, carry):
        total = mm(b["g"][0], b["w"][c, :, 0:DM], 1, 1)
        for i in range(1, M):
            total = total + mm(b["g"][i], b["w"][c, :, i * DM : (i + 1) * DM], 1, 1)
        b["dn"][c] = total
        return carry

    lax.fori_loop(0, NC, grow, 0)

    def place(a, c):
        for t in range(1, D):
            r_copies[a, c, t].wait_recv()
        parts = b["arr"][a, c].reshape(D * CP, CW)
        b["f"][a, c] = mm(b["pick"][...], parts, 1, 0).astype(BF16)

    for c in range(NC):
        place(K, c)
        place(V, c)
        for h in range(HC):
            cols = slice(h * HS, (h + 1) * HS)
            b["lf"][:, cols] = mm(b["f"][K, c, :, cols] * b["mk"][TAIL], b["f"][V, c, :, cols], 0, 0)
        copy = remote(
            b["ls"].at[c], b["st"].at[c], b["f_ss"].at[c], b["f_rs"].at[c], seq=lax.rem(s + 1, S)
        )
        pl.when(s > 0)(copy.wait_recv)
        join = jnp.broadcast_to(b["jn"][0][0:1, 0:1], (HS, CW))
        b["ls"][c] = (b["lf"][...] + jnp.where(join > 0.5, b["st"][c].astype(F32), 0.0)).astype(BF16)
        go(copy, s < S - 1)

    for copy in g_copies:
        copy.wait_recv()
    b_copies = []
    part = b["gz"].at[:, :, px, pl.ds(off, RP), :]
    for t in range(1, M):
        copy = remote(part, part, b["b_ss"].at[t - 1], b["b_rs"].at[t - 1], mp=lax.rem(m + t, M))
        go(copy)
        b_copies.append(copy)

    v_copies = []
    outs = []

    def write(index, c, src, out):
        copy = pltpu.make_async_copy(src, out.at[:, pl.ds(c * CW, CW)], b["o_s"].at[index, c])
        copy.start()
        outs.append(copy)

    def spread(c, origin, right, left):
        block = b["nb"].at[c, origin, co]
        if right is not None:
            go(remote(block, block, b["nr_ss"].at[c, origin], b["n_rs"].at[c, origin], dp=jnp.minimum(d + 1, D - 1)), right)
        if left is not None:
            go(remote(block, block, b["nl_ss"].at[c, origin], b["n_rs"].at[c, origin], dp=jnp.maximum(d - 1, 0)), left)

    def share(c, origin, cond):
        block = b["nb"].at[c, origin, co]
        go(remote(block, block, b["p_ss"].at[c, origin], b["p_rs"].at[c, origin], seq=xi * 2 + 1 - co), cond)

    for c in range(NC):
        place(Q, c)
        for h in range(HC):
            cols = slice(h * HS, (h + 1) * HS)
            q, k, v = (b["f"][a, c, :, cols] for a in (Q, K, V))
            p = (mm(q, k, 1, 1) * b["doc"][...]).astype(BF16)
            b["pm"][c, :, cols] = p
            wide = jnp.concatenate([p, q * b["mk"][CAR]], axis=1)
            attn = mm(wide, jnp.concatenate([v, b["st"][c, :, cols]], axis=0), 1, 0)
            gain_h = gain[:, (c * HC + h) * HS : (c * HC + h + 1) * HS]
            scale = lax.rsqrt(jnp.mean(attn * attn, axis=-1, keepdims=True) + NORM_EPS)
            unit = attn * scale
            b["nb"][c, d, co, :, cols] = (unit * gain_h).astype(BF16)
            g = b["dn"][c, :, cols] * gain_h
            d_attn = scale * (g - unit * jnp.mean(g * unit, axis=-1, keepdims=True))
            d_half = d_attn.astype(BF16)
            b["dh"][c, :, cols] = d_half
        spread(c, d, d < D - 1, d > 0)
        share(c, d, None)
        write(0, c, b["nb"].at[c, d, co], normed_out)
        for h in range(HC):
            cols = slice(h * HS, (h + 1) * HS)
            b["rf"][c, :, cols] = mm(b["f"][Q, c, :, cols] * b["mk"][HEAD], b["dh"][c, :, cols], 0, 0)
        copy = remote(
            b["lr"].at[c], b["rst"].at[c], b["v_ss"].at[c], b["v_rs"].at[c], seq=lax.rem(s + S - 1, S)
        )
        v_copies.append(copy)

        @pl.when(s == S - 1)
        def _(copy=copy, c=c):
            b["lr"][c] = b["rf"][c].astype(BF16)
            copy.start()

    def pass_on(c):
        copy = v_copies[c]

        @pl.when(s < S - 1)
        def _():
            copy.wait_recv()
            join = jnp.broadcast_to(b["jn"][1][0:1, 0:1], (HS, CW))
            b["lr"][c] = (b["rf"][c] + jnp.where(join > 0.5, b["rst"][c].astype(F32), 0.0)).astype(BF16)

        pl.when((s < S - 1) & (s > 0))(copy.start)
        sent.append((s > 0, copy))

    def arrived(c, origin):
        block = b["nb"].at[c, origin, co]
        remote(block, block, b["nr_ss"].at[c, origin], b["n_rs"].at[c, origin], dp=lax.rem(d + 1, D)).wait_recv()

    def relay(c, step):
        @pl.when(d - step >= 0)
        def _():
            arrived(c, d - step)

        spread(c, jnp.maximum(d - step, 0), (d - step >= 0) & (d < D - 1), None)
        share(c, jnp.maximum(d - step, 0), d - step >= 0)

        @pl.when(d + step < D)
        def _():
            arrived(c, d + step)

        spread(c, jnp.minimum(d + step, D - 1), None, (d + step < D) & (d > 0))
        share(c, jnp.minimum(d + step, D - 1), d + step < D)

    def backward(c):
        for h in range(HC):
            cols = slice(h * HS, (h + 1) * HS)
            q, k, v = (b["f"][a, c, :, cols] for a in (Q, K, V))
            dh, p = b["dh"][c, :, cols], b["pm"][c, :, cols]
            st, rst = b["st"][c, :, cols], b["rst"][c, :, cols]
            dp = (mm(dh, v, 1, 1) * b["doc"][...]).astype(BF16)
            rev = b["mk"][REV]
            b["do"][0, c, :, cols] = (mm(dp, k, 1, 0) + mm(dh * b["mk"][CAR], st, 1, 1)).astype(BF16)
            b["do"][1, c, :, cols] = (mm(dp, q, 0, 0) + mm(v * rev, rst, 1, 1)).astype(BF16)
            b["do"][2, c, :, cols] = (mm(p, dh, 0, 0) + mm(k * rev, rst, 1, 0)).astype(BF16)
        for i, out in enumerate((dq_out, dk_out, dv_out)):
            write(1 + i, c, b["do"].at[i, c], out)

    x_copies = {}

    def weigh(c):
        mate = 1 - co
        for o in range(D):
            block = b["nb"].at[c, o, mate]
            remote(block, block, b["p_ss"].at[c, o], b["p_rs"].at[c, o], seq=xi * 2 + 1 - co).wait_recv()
        right = b["nb"][c].reshape(D * 2 * R, CW)
        for t in list(range(1, X)) + [0]:
            to = lax.rem(xi + t, X)
            part = mm(b["lhs"][to], right, 1, 0)
            if t == 0:
                b["acc"][c] = part
                continue
            b["xs"][c, t - 1] = part.astype(BF16)
            copy = remote(
                b["xs"].at[c, t - 1],
                b["xr"].at[c, t - 1],
                b["x_ss"].at[c, t - 1],
                b["x_rs"].at[c, t - 1],
                seq=to * 2 + co,
            )
            go(copy)
            x_copies[c, t] = copy

    def settle(c):
        for t in range(1, X):
            x_copies[c, t].wait_recv()
            b["acc"][c] = b["acc"][c] + b["xr"][c, t - 1].astype(F32)
        write(4, c, b["acc"].at[c], wg_out)

    for c in range(NC):
        pass_on(c)
        if D > 1:
            relay(c, 1)
    for copy in b_copies:
        copy.wait_recv()
    for o in range(D):
        for cc in range(2):
            at = (o * 2 + cc) * R
            b["lhs"][:, :, at : at + R] = b["gz"][o, cc]
    for c in range(NC):
        backward(c)
        if D > 2:
            relay(c, 2)
    for step in range(3, D - 1):
        for c in range(NC):
            relay(c, step)
    for c in range(NC):
        if D > 3:
            relay(c, D - 1)
        weigh(c)
        if c:
            settle(c - 1)
    settle(NC - 1)
    for copy in outs:
        copy.wait()
    for cond, copy in sent:
        when(cond, copy.wait_send)


def solution(mesh):
    def local(queries, key_rows, value_rows, row_plan, segments, norm_gain, out_weight, out_grad):
        rows, width = queries.shape
        z = plan_sizes(mesh, rows, width, out_grad.shape[1])
        scratch = scratch_of(z)
        half = jax.ShapeDtypeStruct((rows, width), BF16)
        anywhere = pl.BlockSpec(memory_space=pl.ANY)
        vmem = pl.BlockSpec(memory_space=pltpu.VMEM)
        smem = pl.BlockSpec(memory_space=pltpu.SMEM)
        return pl.pallas_call(
            functools.partial(whole_body, z, tuple(scratch)),
            out_shape=[half, half, half, half, jax.ShapeDtypeStruct((z["RB"], width), F32)],
            in_specs=[smem, vmem, vmem] + [anywhere] * 5,
            out_specs=[anywhere] * 5,
            scratch_shapes=list(scratch.values()),
            compiler_params=pltpu.CompilerParams(
                collective_id=0, has_side_effects=True, vmem_limit_bytes=60 * 1024 * 1024
            ),
        )(row_plan, segments, norm_gain.reshape(1, width), queries, key_rows, value_rows, out_weight, out_grad)

    placed = (
        P(("dp", "seq"), "mp"),
        P(("dp", "seq"), "mp"),
        P(("dp", "seq"), "mp"),
        P(),
        P("dp", "seq"),
        P("mp"),
        P("mp", None),
        P(("dp", "seq"), "mp"),
    )
    return jax.shard_map(
        local, mesh=mesh, in_specs=placed, out_specs=(P(("dp", "seq"), "mp"),) * 5, check_vma=False
    )
```

time: 223 us -> 117 us (0.52)
  waiting for transfers between devices: 90.5 us -> 0 us
  Pallas kernels: 19.8 us -> 109 us
  starting transfers between devices: 24.9 us -> 0 us
  other arithmetic: 21.7 us -> 0 us
  matrix products: 21.2 us -> 0 us
  blocking collectives: 18.4 us -> 0 us
  between operations: 17.3 us -> 0.66 us
    pallas_call x3 -> x1, Pallas kernels: 19.8 us -> 109 us  [local(): pl.pallas_call(functools.partial(whole_body, z, tuple(scratch)), out_shap...]
    all_gather x1 -> x0, waiting for transfers between devices: 44.8 us -> none  [local(): everyone = lax.all_gather(normed, ('dp', 'seq'), axis=0)]
    all_to_all x4 -> x0, waiting for transfers between devices: 32.6 us -> none  [the longest x3 26.2 us: hand(): return lax.all_to_all(packed, 'dp', split_axis=0, concat_axis=0, tiled=True)]
    dot_general x5 -> x0, matrix products: 21.2 us -> none  [the longest x1 9.8 us: local(): lax.dot_general(full_grad, out_weight, (((1,), (1,)), ((), ())), preferre...]
    all_to_all x4 -> x0, starting transfers between devices: 18.7 us -> none  [the longest x3 13.3 us: hand(): return lax.all_to_all(packed, 'dp', split_axis=0, concat_axis=0, tiled=True)]
    ppermute x6 -> x0, waiting for transfers between devices: 13.1 us -> none  [chain(): got = got + lax.ppermute(sent.astype(BF16), axis, [(at, at + step)])]
    convert_element_type x10 -> x0, other arithmetic: 12.4 us -> none  [the longest x6 8.4 us: chain(): got = got + lax.ppermute(sent.astype(BF16), axis, [(at, at + step)])]
    all_gather x1 -> x0, blocking collectives: 12.2 us -> none  [local(): full_grad = lax.all_gather(out_grad, 'mp', axis=1, tiled=True)]
  transfers between devices with their start and end apart: 11 -> 0, of which waited for: 7 -> 0; matrix products, arithmetic and copies ran while one was open for 16% -> 0% of each run, Pallas kernels for 3% -> 0%
where the time goes in v1:
time: 117 us
  Pallas kernels  109 us (93%)
  local copies, waits for them, and re-layouts  6.71 us (6%)
    pallas_call x1, Pallas kernels, local(): pl.pallas_call(functools.partial(whole_body, z, tuple(scratch)), out_shap...  109 us
    unnamed x11, local copies, waits for them, and re-layouts  6.71 us

profile of v1, /device:TPU:0, one launch (start us, length us, event | category | flops | bytes accessed | tf_op | source)
XLA Modules:
  0.0 116.6 jit_solution(9414648337525262706)
XLA Ops:
  0.6 109.2 %shard_map.119 = (bf16[128,2048]{1,0:T(8,128)(2,1)}, bf16[128,2048]{1,0:T(8,128)(2,1)}, bf16[128,2048]{1,0:T(8,128)(2,1)}, bf16[128,2048]{1,0:T(8,128)(2,1)}, f32[192,2048]{1,0:T(8,128)}) custom-call(s32[4,4]{1,0:T(4,128)} %refs_0_.1, s32[1,128]{1,0:T(1,128)} %refs_1_.1, f32[1,2048]{1,0:T(1,128)} %bitcast.1, bf16[128,2048]{1,0:T(8,128)(2,1)} %refs_3_.1, ...), custom_call_target="tpu_custom_call" | custom-call | tf_op jit(solution)/shard_map/pallas_call | solution.py:489
  109.9 0.0 copy-start.2
  109.9 0.0 copy-start.1
  109.9 2.0 %copy.18 = bf16[128,2048]{1,0:T(8,128)(2,1)} copy(bf16[128,2048]{1,0:T(8,128)(2,1)} %get-tuple-element.10) | data formatting | bytes 1048576
  111.9 0.0 copy-start
  111.9 2.0 %copy.19 = bf16[128,2048]{1,0:T(8,128)(2,1)} copy(bf16[128,2048]{1,0:T(8,128)(2,1)} %get-tuple-element.11) | data formatting | bytes 1048576
  113.9 0.0 copy-done.2
  113.9 0.8 copy.20
  114.7 0.0 copy-done.1
  114.7 0.8 copy.21
  115.4 0.0 copy-done
  115.5 1.1 copy.22
Async XLA Ops:
  109.9 4.0 %copy-start.2 = (bf16[128,2048]{1,0:T(8,128)(2,1)S(1)}, bf16[128,2048]{1,0:T(8,128)(2,1)}, u32[]{:S(2)}) copy-start(bf16[128,2048]{1,0:T(8,128)(2,1)} %get-tuple-element.12) | copy-start | bytes 1572868
  109.9 4.8 %copy-start.1 = (bf16[128,2048]{1,0:T(8,128)(2,1)S(1)}, bf16[128,2048]{1,0:T(8,128)(2,1)}, u32[]{:S(2)}) copy-start(bf16[128,2048]{1,0:T(8,128)(2,1)} %get-tuple-element.13) | copy-start | bytes 1572868
  111.9 3.6 %copy-start = (f32[192,2048]{1,0:T(8,128)S(1)}, f32[192,2048]{1,0:T(8,128)}, u32[]{:S(2)}) copy-start(f32[192,2048]{1,0:T(8,128)} %get-tuple-element.14) | copy-start | bytes 4718596

commit v2 on v1

--- a/solution.py
+++ b/solution.py
@@ -51,7 +51,9 @@
         g=vm((M, R, z["DM"]), BF16),
         gt=vm((z["DOUT"], R), BF16),
         gz=vm((D, 2, X, z["RB"], R), BF16),
-        lhs=vm((X, z["RB"], D * 2 * R), BF16),
+        plan=pltpu.SMEM((D, D), jnp.int32),
+        segi=vm((1, R), jnp.int32),
+        gain=vm((1, W), F32),
         dn=vm((NC, R, CW), F32),
         pm=vm((NC, R, CW), BF16),
         lf=vm((HS, CW), F32),
@@ -62,8 +64,7 @@
         rst=vm((NC, HS, CW), BF16),
         dh=vm((NC, R, CW), BF16),
         nb=vm((NC, D, 2, R, CW), BF16),
-        do=vm((3, NC, R, CW), BF16),
-        acc=vm((NC, z["RB"], CW), F32),
+        acc=vm((NC, X, z["RB"], CW), F32),
         xs=vm((NC, XO, z["RB"], CW), BF16),
         xr=vm((NC, XO, z["RB"], CW), BF16),
         seg=vm((3, 8, R), F32),
@@ -72,7 +73,7 @@
         jn=vm((2, 8, R), F32),
         sel=vm((D * z["CP"], R), BF16),
         pick=vm((R, D * z["CP"]), BF16),
-        in_s=dma((4,)),
+        in_s=dma((7,)),
         w_s=dma((NC,)),
         y_ss=dma((max(1, M - 1),)),
         y_rs=dma((max(1, M - 1),)),
@@ -93,9 +94,8 @@
         n_rs=dma((NC, D)),
         p_ss=dma((NC, D)),
         p_rs=dma((NC, D)),
-        x_ss=dma((NC, XO)),
-        x_rs=dma((NC, XO)),
-        o_s=dma((5, NC)),
+        x_ss=dma((NC, XO, 2)),
+        x_rs=dma((NC, XO, 2)),
     )
 
 
@@ -103,9 +103,10 @@
 
 
 def whole_body(z, names, *refs):
-    plan, seg_in, gain, q_in, k_in, v_in, w_in, g_in = refs[:8]
-    normed_out, dq_out, dk_out, dv_out, wg_out = refs[8:13]
-    b = dict(zip(names, refs[13:]))
+    plan_in, seg_in, gain_in, q_in, k_in, v_in, w_in, g_in = refs[:8]
+    normed_out, grads_out, wg_out = refs[8:11]
+    b = dict(zip(names, refs[11:]))
+    plan, gain = b["plan"], b["gain"]
     D, S, M, X, R, NC, CW, HC = (z[n] for n in ("D", "S", "M", "X", "R", "NC", "CW", "HC"))
     CAP, CP, RB, RP, PX, DM = (z[n] for n in ("CAP", "CP", "RB", "RP", "PX", "DM"))
     d, s, m = lax.axis_index("dp"), lax.axis_index("seq"), lax.axis_index("mp")
@@ -127,17 +128,29 @@
         when(cond, copy.start)
         sent.append((cond, copy))
 
-    sources = ((k_in, b["x"].at[K]), (v_in, b["x"].at[V]), (q_in, b["x"].at[Q]), (g_in, b["g"].at[m]))
+    barrier = pltpu.get_barrier_semaphore()
+    peers = 0
+
+    def greet(**where):
+        pl.semaphore_signal(barrier, inc=1, device_id=where, device_id_type=MESH)
+
+    sources = (
+        (plan_in, plan),
+        (k_in, b["x"].at[K]),
+        (v_in, b["x"].at[V]),
+        (g_in, b["g"].at[m]),
+        (seg_in, b["segi"]),
+        (q_in, b["x"].at[Q]),
+        (gain_in, gain),
+    )
     loads = [pltpu.make_async_copy(a, c, b["in_s"].at[i]) for i, (a, c) in enumerate(sources)]
-    for i in (0, 3, 1, 2):
-        loads[i].start()
+    for load in loads:
+        load.start()
     w_loads = [
         pltpu.make_async_copy(w_in.at[pl.ds(c * CW, CW), :], b["w"].at[c], b["w_s"].at[c])
         for c in range(NC)
     ]
 
-    own_seg = seg_in[...].astype(F32)
-    b["seg"][0] = jnp.broadcast_to(own_seg, (8, R))
     if CP > CAP:
         b["arr"][:, :, :, CAP:CP, :] = jnp.zeros((3, NC, D, CP - CAP, CW), BF16)
 
@@ -150,12 +163,6 @@
     def _():
         b["seg"][2] = jnp.full((8, R), -1.0, F32)
         b["rst"][...] = jnp.zeros_like(b["rst"])
-
-    barrier = pltpu.get_barrier_semaphore()
-    peers = 0
-
-    def greet(**where):
-        pl.semaphore_signal(barrier, inc=1, device_id=where, device_id_type=MESH)
 
     for t in range(D):
         for cc in range(2):
@@ -170,6 +177,7 @@
         greet(dp=d, seq=s, mp=lax.rem(m + t, M))
         peers += 1
 
+    loads[0].wait()
     slot = lax.broadcasted_iota(jnp.int32, (D * CP, R), 0)
     row = lax.broadcasted_iota(jnp.int32, (D * CP, R), 1)
     start = jnp.int32(0)
@@ -201,6 +209,8 @@
         )
         go(c)
         y_copies.append(c)
+    loads[4].wait()
+    b["seg"][0] = jnp.broadcast_to(b["segi"][...].astype(F32), (8, R))
     after = remote(b["seg"].at[0], b["seg"].at[1], b["sg_ss"].at[0], b["sg_rs"].at[0], seq=lax.rem(s + 1, S))
     before = remote(
         b["seg"].at[0], b["seg"].at[2], b["sg_ss"].at[1], b["sg_rs"].at[1], seq=lax.rem(s + S - 1, S)
@@ -226,14 +236,14 @@
             r_copies[a, c, t] = copy
         b["arr"][a, c, d] = b["snd"][a, c, d]
 
-    loads[0].wait()
     loads[1].wait()
+    loads[2].wait()
     for c in range(NC):
         hand(K, c)
         hand(V, c)
     for c in range(NC):
         w_loads[c].start()
-    loads[2].wait()
+    loads[5].wait()
     for c in range(NC):
         hand(Q, c)
 
@@ -310,22 +320,8 @@
         b["ls"][c] = (b["lf"][...] + jnp.where(join > 0.5, b["st"][c].astype(F32), 0.0)).astype(BF16)
         go(copy, s < S - 1)
 
-    for copy in g_copies:
-        copy.wait_recv()
-    b_copies = []
-    part = b["gz"].at[:, :, px, pl.ds(off, RP), :]
-    for t in range(1, M):
-        copy = remote(part, part, b["b_ss"].at[t - 1], b["b_rs"].at[t - 1], mp=lax.rem(m + t, M))
-        go(copy)
-        b_copies.append(copy)
-
     v_copies = []
-    outs = []
-
-    def write(index, c, src, out):
-        copy = pltpu.make_async_copy(src, out.at[:, pl.ds(c * CW, CW)], b["o_s"].at[index, c])
-        copy.start()
-        outs.append(copy)
+    loads[6].wait()
 
     def spread(c, origin, right, left):
         block = b["nb"].at[c, origin, co]
@@ -350,14 +346,15 @@
             gain_h = gain[:, (c * HC + h) * HS : (c * HC + h + 1) * HS]
             scale = lax.rsqrt(jnp.mean(attn * attn, axis=-1, keepdims=True) + NORM_EPS)
             unit = attn * scale
-            b["nb"][c, d, co, :, cols] = (unit * gain_h).astype(BF16)
+            out = (unit * gain_h).astype(BF16)
+            b["nb"][c, d, co, :, cols] = out
+            normed_out[c, :, cols] = out
             g = b["dn"][c, :, cols] * gain_h
             d_attn = scale * (g - unit * jnp.mean(g * unit, axis=-1, keepdims=True))
             d_half = d_attn.astype(BF16)
             b["dh"][c, :, cols] = d_half
         spread(c, d, d < D - 1, d > 0)
         share(c, d, None)
-        write(0, c, b["nb"].at[c, d, co], normed_out)
         for h in range(HC):
             cols = slice(h * HS, (h + 1) * HS)
             b["rf"][c, :, cols] = mm(b["f"][Q, c, :, cols] * b["mk"][HEAD], b["dh"][c, :, cols], 0, 0)
@@ -410,71 +407,120 @@
             st, rst = b["st"][c, :, cols], b["rst"][c, :, cols]
             dp = (mm(dh, v, 1, 1) * b["doc"][...]).astype(BF16)
             rev = b["mk"][REV]
-            b["do"][0, c, :, cols] = (mm(dp, k, 1, 0) + mm(dh * b["mk"][CAR], st, 1, 1)).astype(BF16)
-            b["do"][1, c, :, cols] = (mm(dp, q, 0, 0) + mm(v * rev, rst, 1, 1)).astype(BF16)
-            b["do"][2, c, :, cols] = (mm(p, dh, 0, 0) + mm(k * rev, rst, 1, 0)).astype(BF16)
-        for i, out in enumerate((dq_out, dk_out, dv_out)):
-            write(1 + i, c, b["do"].at[i, c], out)
+            grads_out[0, c, :, cols] = (mm(dp, k, 1, 0) + mm(dh * b["mk"][CAR], st, 1, 1)).astype(BF16)
+            grads_out[1, c, :, cols] = (mm(dp, q, 0, 0) + mm(v * rev, rst, 1, 1)).astype(BF16)
+            grads_out[2, c, :, cols] = (mm(p, dh, 0, 0) + mm(k * rev, rst, 1, 0)).astype(BF16)
+
+    def add(c, origin, t, cols, fresh=False):
+        to = lax.rem(xi + t, X)
+        left = jnp.concatenate([b["gz"][origin, 0, to], b["gz"][origin, 1, to]], axis=1)
+        right = b["nb"][c, origin, :, :, cols].reshape(2 * R, cols.stop - cols.start)
+        term = mm(left, right, 1, 0)
+        b["acc"][c, t, :, cols] = term if fresh else b["acc"][c, t, :, cols] + term
+
+    everything = slice(0, CW)
+    pieces = (slice(0, CW // 2), slice(CW // 2, CW)) if CW % (2 * HS) == 0 else (everything,)
+
+    def paired(c, origin):
+        block = b["nb"].at[c, origin, 1 - co]
+        remote(block, block, b["p_ss"].at[c, origin], b["p_rs"].at[c, origin], seq=xi * 2 + 1 - co).wait_recv()
+
+    def each(step, act):
+        if step == 0:
+            act(d)
+            return
+        pl.when(d - step >= 0)(lambda: act(d - step))
+        pl.when(d + step < D)(lambda: act(d + step))
+
+    def absorb(c, step):
+        def one(origin):
+            paired(c, origin)
+            for t in range(X):
+                add(c, origin, t, everything, fresh=step == 0)
+
+        each(step, one)
 
     x_copies = {}
 
-    def weigh(c):
-        mate = 1 - co
-        for o in range(D):
-            block = b["nb"].at[c, o, mate]
-            remote(block, block, b["p_ss"].at[c, o], b["p_rs"].at[c, o], seq=xi * 2 + 1 - co).wait_recv()
-        right = b["nb"][c].reshape(D * 2 * R, CW)
+    def close(c, step):
+        each(step, lambda origin: paired(c, origin))
         for t in list(range(1, X)) + [0]:
-            to = lax.rem(xi + t, X)
-            part = mm(b["lhs"][to], right, 1, 0)
-            if t == 0:
-                b["acc"][c] = part
-                continue
-            b["xs"][c, t - 1] = part.astype(BF16)
-            copy = remote(
-                b["xs"].at[c, t - 1],
-                b["xr"].at[c, t - 1],
-                b["x_ss"].at[c, t - 1],
-                b["x_rs"].at[c, t - 1],
-                seq=to * 2 + co,
-            )
-            go(copy)
-            x_copies[c, t] = copy
+            for i, cols in enumerate(pieces):
+                each(step, lambda origin: add(c, origin, t, cols, fresh=step == 0))
+                if t == 0:
+                    continue
+                b["xs"][c, t - 1, :, cols] = b["acc"][c, t, :, cols].astype(BF16)
+                part = pl.ds(cols.start, cols.stop - cols.start)
+                copy = remote(
+                    b["xs"].at[c, t - 1, :, part],
+                    b["xr"].at[c, t - 1, :, part],
+                    b["x_ss"].at[c, t - 1, i],
+                    b["x_rs"].at[c, t - 1, i],
+                    seq=lax.rem(xi + t, X) * 2 + co,
+                )
+                go(copy)
+                x_copies[c, t, i] = copy
 
     def settle(c):
-        for t in range(1, X):
-            x_copies[c, t].wait_recv()
-            b["acc"][c] = b["acc"][c] + b["xr"][c, t - 1].astype(F32)
-        write(4, c, b["acc"].at[c], wg_out)
+        for i, cols in enumerate(pieces):
+            total = b["acc"][c, 0, :, cols]
+            for t in range(1, X):
+                x_copies[c, t, i].wait_recv()
+                total = total + b["xr"][c, t - 1, :, cols].astype(F32)
+            wg_out[c, :, cols] = total
+
+    for copy in g_copies:
+        copy.wait_recv()
+    b_copies = []
+    part = b["gz"].at[:, :, px, pl.ds(off, RP), :]
+    for t in range(1, M):
+        copy = remote(part, part, b["b_ss"].at[t - 1], b["b_rs"].at[t - 1], mp=lax.rem(m + t, M))
+        go(copy)
+        b_copies.append(copy)
 
     for c in range(NC):
         pass_on(c)
+    for c in range(NC):
         if D > 1:
             relay(c, 1)
+        backward(c)
     for copy in b_copies:
         copy.wait_recv()
-    for o in range(D):
-        for cc in range(2):
-            at = (o * 2 + cc) * R
-            b["lhs"][:, :, at : at + R] = b["gz"][o, cc]
-    for c in range(NC):
-        backward(c)
-        if D > 2:
-            relay(c, 2)
-    for step in range(3, D - 1):
+    last = D - 1
+    for step in range(2, last):
         for c in range(NC):
             relay(c, step)
-    for c in range(NC):
-        if D > 3:
-            relay(c, D - 1)
-        weigh(c)
+            if step == 2:
+                absorb(c, 0)
+            absorb(c, step - 1)
+    for c in range(NC):
+        if last > 1:
+            relay(c, last)
+        if last in (1, 2):
+            absorb(c, 0)
+        if last > 1:
+            absorb(c, last - 1)
+        close(c, last)
         if c:
             settle(c - 1)
     settle(NC - 1)
-    for copy in outs:
-        copy.wait()
     for cond, copy in sent:
         when(cond, copy.wait_send)
+
+
+def write_body(n_chunks, normed, grads, wg, *refs):
+    outs, sem = refs[:5], refs[5]
+    width = normed.shape[2]
+    copies = []
+    for c in range(n_chunks):
+        cols = pl.ds(c * width, width)
+        parts = (normed.at[c], grads.at[0, c], grads.at[1, c], grads.at[2, c], wg.at[c])
+        for i, (part, out) in enumerate(zip(parts, outs)):
+            copies.append(pltpu.make_async_copy(part, out.at[:, cols], sem.at[c, i]))
+    for copy in copies:
+        copy.start()
+    for copy in copies:
+        copy.wait()
 
 
 def solution(mesh):
@@ -482,20 +528,42 @@
         rows, width = queries.shape
         z = plan_sizes(mesh, rows, width, out_grad.shape[1])
         scratch = scratch_of(z)
-        half = jax.ShapeDtypeStruct((rows, width), BF16)
+        chunks, span = z["NC"], z["CW"]
         anywhere = pl.BlockSpec(memory_space=pl.ANY)
         vmem = pl.BlockSpec(memory_space=pltpu.VMEM)
-        smem = pl.BlockSpec(memory_space=pltpu.SMEM)
-        return pl.pallas_call(
+        operands = (
+            row_plan,
+            segments,
+            norm_gain.reshape(1, width),
+            queries,
+            key_rows,
+            value_rows,
+            out_weight,
+            out_grad,
+        )
+        kept = pl.pallas_call(
             functools.partial(whole_body, z, tuple(scratch)),
-            out_shape=[half, half, half, half, jax.ShapeDtypeStruct((z["RB"], width), F32)],
-            in_specs=[smem, vmem, vmem] + [anywhere] * 5,
-            out_specs=[anywhere] * 5,
+            out_shape=[
+                pltpu.VMEM((chunks, rows, span), BF16),
+                pltpu.VMEM((3, chunks, rows, span), BF16),
+                pltpu.VMEM((chunks, z["RB"], span), F32),
+            ],
+            in_specs=[pl.BlockSpec(memory_space=pltpu.HBM)] * 8,
+            out_specs=[vmem] * 3,
             scratch_shapes=list(scratch.values()),
             compiler_params=pltpu.CompilerParams(
-                collective_id=0, has_side_effects=True, vmem_limit_bytes=60 * 1024 * 1024
+                collective_id=0, has_side_effects=True, vmem_limit_bytes=50 * 1024 * 1024
             ),
-        )(row_plan, segments, norm_gain.reshape(1, width), queries, key_rows, value_rows, out_weight, out_grad)
+        )(*(pltpu.with_memory_space_constraint(a, pltpu.HBM) for a in operands))
+        half = jax.ShapeDtypeStruct((rows, width), BF16)
+        return pl.pallas_call(
+            functools.partial(write_body, chunks),
+            out_shape=[half, half, half, half, jax.ShapeDtypeStruct((z["RB"], width), F32)],
+            in_specs=[anywhere] * 3,
+            out_specs=[anywhere] * 5,
+            scratch_shapes=[pltpu.SemaphoreType.DMA((chunks, 5))],
+            compiler_params=pltpu.CompilerParams(vmem_limit_bytes=4 * 1024 * 1024),
+        )(*kept)
 
     placed = (
         P(("dp", "seq"), "mp"),

time: 117 us -> 107 us (0.915)
  local copies, waits for them, and re-layouts: 6.71 us -> 0 us
  Pallas kernels: 109 us -> 106 us
    unnamed x11 -> x0, local copies, waits for them, and re-layouts: 6.71 us -> none
    pallas_call x1, Pallas kernels: 109 us -> 104 us  [local(): pl.pallas_call(functools.partial(whole_body, z, tuple(scratch)), out_shap...]
    pallas_call x0 -> x1, Pallas kernels: none -> 2 us  [local(): pl.pallas_call(functools.partial(write_body, chunks), out_shape=[half, ha...]
where the time goes in v2:
time: 107 us
  Pallas kernels  106 us (99%)
    pallas_call x1, Pallas kernels, local(): pl.pallas_call(functools.partial(whole_body, z, tuple(scratch)), out_shap...  104 us

profile of v2, /device:TPU:0, one launch (start us, length us, event | category | flops | bytes accessed | tf_op | source)
XLA Modules:
  0.0 106.9 jit_solution(11953000129566457571)
XLA Ops:
  0.6 104.1 %shard_map.119 = (bf16[4,128,512]{2,1,0:T(8,128)(2,1)S(1)}, bf16[3,4,128,512]{3,2,1,0:T(8,128)(2,1)S(1)}, f32[4,192,512]{2,1,0:T(8,128)S(1)}) custom-call(s32[4,4]{1,0:T(4,128)} %refs_0_.1, s32[1,128]{1,0:T(1,128)} %refs_1_.1, f32[1,2048]{1,0:T(1,128)} %bitcast.1, bf16[128,2048]{1,0:T(8,128)(2,1)} %refs_3_.1, bf16[128,2048]{1,0:T(8,128)(2,1)} %refs_4_.1, ...), custom_call_target="tpu_custom_call" | custom-call | tf_op jit(solution)/shard_map/pallas_call | solution.py:544
  104.7 2.0 %shard_map.120 = (bf16[128,2048]{1,0:T(8,128)(2,1)}, bf16[128,2048]{1,0:T(8,128)(2,1)}, bf16[128,2048]{1,0:T(8,128)(2,1)}, bf16[128,2048]{1,0:T(8,128)(2,1)}, f32[192,2048]{1,0:T(8,128)}) custom-call(bf16[4,128,512]{2,1,0:T(8,128)(2,1)S(1)} %get-tuple-element.8.normed, bf16[3,4,128,512]{3,2,1,0:T(8,128)(2,1)S(1)} %get-tuple-element.9.grads, ...), custom_call_target="tpu_custom_call" | custom-call | tf_op jit(solution)/shard_map/pallas_call | solution.py:559

commit v3 on v2

v3 whole, which is shorter than its diff:
```python
import functools

import jax
import jax.numpy as jnp
from jax import lax
from jax.experimental import pallas as pl
from jax.experimental.pallas import tpu as pltpu
from jax.sharding import PartitionSpec as P

HS = 128
NORM_EPS = 1e-06
F32 = jnp.float32
BF16 = jnp.bfloat16
MESH = pl.DeviceIdType.MESH
K, V, Q = 0, 1, 2
SPAN = 4
TERMS = 1
STEP = 2


def mm(a, b, ca, cb):
    return lax.dot_general(a, b, (((ca,), (cb,)), ((), ())), preferred_element_type=F32)


def plan_sizes(mesh, rows, width, out_half):
    groups, shards, splits = mesh.shape["dp"], mesh.shape["seq"], mesh.shape["mp"]
    z = {}
    z["D"], z["S"], z["M"], z["X"] = groups, shards, splits, shards // 2
    z["R"], z["W"], z["DM"] = rows, width, out_half
    z["DOUT"] = out_half * splits
    heads = width // HS
    full, rest = divmod(heads, SPAN)
    z["HEADS"] = [SPAN] * full + [rest] * (rest > 0)
    z["NC"] = len(z["HEADS"])
    z["CW"] = max(z["HEADS"]) * HS
    z["CAP"] = rows // min(groups, 8) + rows // 16
    z["CP"] = -(-z["CAP"] // 16) * 16
    z["RB"] = z["DOUT"] // (groups * shards)
    z["PX"] = splits // z["X"]
    z["RP"] = z["RB"] // z["PX"]
    return z


def scratch_of(z):
    D, M, X, R, W, NC, CW = (z[n] for n in ("D", "M", "X", "R", "W", "NC", "CW"))
    XO, SO = max(1, X - 1), max(1, z["S"] - 1)
    vm = pltpu.VMEM
    dma = pltpu.SemaphoreType.DMA
    return dict(
        x=vm((3, R, W), BF16),
        snd=vm((3, NC, D, z["CP"], CW), BF16),
        arr=vm((3, NC, D, z["CP"], CW), BF16),
        f=vm((3, NC, R, CW), BF16),
        w=vm((NC, CW, z["DOUT"]), BF16),
        g=vm((M, R, z["DM"]), BF16),
        gt=vm((z["DOUT"], R), BF16),
        gz=vm((D, 2, X, z["RB"], R), BF16),
        plan=pltpu.SMEM((D, D), jnp.int32),
        segi=vm((1, R), jnp.int32),
        gain=vm((1, W), F32),
        dn=vm((NC, R, CW), F32),
        pm=vm((NC, R, CW), BF16),
        tot=vm((HS, CW), F32),
        ls=vm((NC, HS, CW), BF16),
        sr=vm((NC, SO, HS, CW), BF16),
        st=vm((NC, HS, CW), BF16),
        lr=vm((NC, HS, CW), BF16),
        rr=vm((NC, SO, HS, CW), BF16),
        rst=vm((NC, HS, CW), BF16),
        dh=vm((NC, R, CW), BF16),
        nb=vm((NC, D, 2, R, CW), BF16),
        acc=vm((NC, X, z["RB"], CW), F32),
        xs=vm((NC, XO, z["RB"], CW), BF16),
        xr=vm((NC, XO, z["RB"], CW), BF16),
        seg=vm((2 * SO + 1, 8, R), F32),
        doc=vm((R, R), F32),
        mk=vm((4, R, R), BF16),
        jn=vm((2 * SO, 8, R), F32),
        sel=vm((D * z["CP"], R), BF16),
        pick=vm((R, D * z["CP"]), BF16),
        in_s=dma((7,)),
        w_s=dma((NC,)),
        y_ss=dma((max(1, M - 1),)),
        y_rs=dma((max(1, M - 1),)),
        sg_ss=dma((2 * SO,)),
        sg_rs=dma((2 * SO,)),
        r_ss=dma((3, NC, D)),
        r_rs=dma((3, NC, D)),
        g_ss=dma((2 * D,)),
        g_rs=dma((2 * D,)),
        b_ss=dma((max(1, M - 1),)),
        b_rs=dma((max(1, M - 1),)),
        f_ss=dma((NC, SO)),
        f_rs=dma((NC, SO)),
        v_ss=dma((NC, SO)),
        v_rs=dma((NC, SO)),
        nr_ss=dma((NC, D)),
        nl_ss=dma((NC, D)),
        n_rs=dma((NC, D)),
        p_ss=dma((NC, D)),
        p_rs=dma((NC, D)),
        x_ss=dma((NC, XO, 2)),
        x_rs=dma((NC, XO, 2)),
    )


TAIL, HEAD, CAR, REV = 0, 1, 2, 3


def order(n, groups):
    last = groups - 1
    steps = []

    def do(name, *args):
        steps.append((name, *args))

    def rows(act, c, *names):
        for a in names if c < n else ():
            do(act, a, c)

    rows("pack", 0, K)
    rows("send", 0, K)
    rows("pack", 0, V)
    rows("send", 0, V)
    do("fetch")
    for c in range(2):
        rows("pack", c + 1, K, V)
        rows("send", c + 1, K, V)
        rows("pack", c, Q)
        rows("send", c, Q)
    do("masks")
    for c in range(2, n):
        rows("pack", c + 1, K, V)
        rows("pack", c, Q)
    do("turn")
    for c in range(min(2, n)):
        do("grow", c)
        do("keep", c)
    early = []
    left = [(STEP * k + c, c, k) for c in range(n) for k in range(1, last + 1)]
    for c in range(n):
        do("forward", c)
        if c == TERMS:
            do("terms")
        rows("send", c + 3, K, V)
        rows("send", c + 2, Q)
        if c + 2 < n:
            do("grow", c + 2)
        if 1 <= c < n - 1 and last:
            do("relay", c - 1, 1)
            left.remove((STEP + c - 1, c - 1, 1))
            early.append((c - 1, 0))
        if c + 2 < n:
            do("keep", c + 2)
        if 2 <= c < n - 1:
            do("backward", c - 2)
    if n <= TERMS:
        do("terms")
    do("double")
    behind, closed, due, ready = list(range(max(0, n - 3), n)), [], early, False

    def finish(c):
        if ("doubled",) not in steps:
            do("doubled")
        for item in [item for item in due if item[0] == c]:
            do("absorb", *item)
            due.remove(item)
        do("close", c)
        closed.append(c)
        if len(closed) > 1:
            do("settle", closed[-2])

    for _, c, k in sorted(left):
        if (c, k) == (n - 1, last):
            while behind:
                do("backward", behind.pop(0))
        do("relay", c, k)
        if (c, k) == (n - 2, 1):
            do("backward", behind.pop(0))
        if (c, k) == (n - 1, 1):
            if ("doubled",) not in steps:
                do("doubled")
            ready = True
        if k == 1:
            due.append((c, 0))
        else:
            due.append((c, k - 1))
        if ready:
            for item in [item for item in due if item[0] == due[0][0] and item[1] < last - 1][:2]:
                do("absorb", *item)
                due.remove(item)
        if (c, k) == (n - 1, last - 1) and behind:
            do("backward", behind.pop(0))
        if k == last:
            finish(c)
    if not last:
        due.extend((c, 0) for c in range(n))
        for c in range(n):
            finish(c)
    while behind:
        do("backward", behind.pop(0))
    if closed:
        do("settle", closed[-1])
    return steps


def whole_body(z, names, *refs):
    plan_in, seg_in, gain_in, q_in, k_in, v_in, w_in, g_in = refs[:8]
    normed_out, grads_out, wg_out = refs[8:11]
    b = dict(zip(names, refs[11:]))
    plan, gain = b["plan"], b["gain"]
    D, S, M, X, R, NC, CW, HEADS = (z[n] for n in ("D", "S", "M", "X", "R", "NC", "CW", "HEADS"))
    first = [sum(HEADS[:c]) for c in range(NC)]
    wide = [count * HS for count in HEADS]
    CAP, CP, RB, RP, PX, DM = (z[n] for n in ("CAP", "CP", "RB", "RP", "PX", "DM"))
    d, s, m = lax.axis_index("dp"), lax.axis_index("seq"), lax.axis_index("mp")
    xi, co = s // 2, s % 2
    sent = []

    def remote(src, dst, ss, rs, **where):
        return pltpu.make_async_remote_copy(
            src_ref=src, dst_ref=dst, send_sem=ss, recv_sem=rs, device_id=where, device_id_type=MESH
        )

    def when(cond, act):
        if cond is None:
            act()
        else:
            pl.when(cond)(act)

    def go(copy, cond=None):
        when(cond, copy.start)
        sent.append((cond, copy))

    barrier = pltpu.get_barrier_semaphore()
    peers = 0

    def greet(**where):
        pl.semaphore_signal(barrier, inc=1, device_id=where, device_id_type=MESH)

    sources = (
        (plan_in, plan),
        (k_in, b["x"].at[K]),
        (v_in, b["x"].at[V]),
        (g_in, b["g"].at[m]),
        (seg_in, b["segi"]),
        (q_in, b["x"].at[Q]),
        (gain_in, gain),
    )
    loads = [pltpu.make_async_copy(a, c, b["in_s"].at[i]) for i, (a, c) in enumerate(sources)]
    for load in loads:
        load.start()
    w_loads = [
        pltpu.make_async_copy(
            w_in.at[pl.ds(first[c] * HS, wide[c]), :], b["w"].at[c, pl.ds(0, wide[c])], b["w_s"].at[c]
        )
        for c in range(NC)
    ]

    def fetch():
        for load in w_loads:
            load.start()

    if CP > CAP:
        b["arr"][:, :, :, CAP:CP, :] = jnp.zeros((3, NC, D, CP - CAP, CW), BF16)

    b["seg"][...] = jnp.full(b["seg"].shape, -1.0, F32)

    for t in range(D):
        for cc in range(2):
            if t or cc:
                greet(dp=lax.rem(d + t, D), seq=xi * 2 + (co + cc) % 2, mp=m)
                peers += 1
    for t in range(1, X):
        for cc in range(2):
            greet(dp=d, seq=lax.rem(xi + t, X) * 2 + cc, mp=m)
            peers += 1
    for t in range(1, M):
        greet(dp=d, seq=s, mp=lax.rem(m + t, M))
        peers += 1

    loads[0].wait()
    slot = lax.broadcasted_iota(jnp.int32, (D * CP, R), 0)
    row = lax.broadcasted_iota(jnp.int32, (D * CP, R), 1)
    start = jnp.int32(0)
    hot = jnp.zeros((D * CP, R), F32)
    for j in range(D):
        inside = (slot >= j * CP) & (slot < j * CP + CAP) & (row - start == slot - j * CP)
        hot = jnp.where(inside, 1.0, hot)
        start = start + plan[d, j]
    b["sel"][...] = hot.astype(BF16)
    slot = lax.broadcasted_iota(jnp.int32, (R, D * CP), 1)
    row = lax.broadcasted_iota(jnp.int32, (R, D * CP), 0)
    start = jnp.int32(0)
    hot = jnp.zeros((R, D * CP), F32)
    for i in range(D):
        count = plan[i, d]
        at = slot - i * CP
        inside = (at >= 0) & (at < CP) & (at == row - start) & (row - start < count)
        hot = jnp.where(inside, 1.0, hot)
        start = start + count
    b["pick"][...] = hot.astype(BF16)

    pl.semaphore_wait(barrier, peers)

    loads[3].wait()
    y_copies = []
    for t in range(1, M):
        c = remote(
            b["g"].at[m], b["g"].at[m], b["y_ss"].at[t - 1], b["y_rs"].at[t - 1], mp=lax.rem(m + t, M)
        )
        go(c)
        y_copies.append(c)
    loads[4].wait()
    b["seg"][0] = jnp.broadcast_to(b["segi"][...].astype(F32), (8, R))
    after, before = {}, {}
    for t in range(1, S):
        near, far = 2 * t - 1, 2 * t
        after[t] = remote(
            b["seg"].at[0], b["seg"].at[near], b["sg_ss"].at[near - 1], b["sg_rs"].at[near - 1], seq=lax.rem(s + t, S)
        )
        before[t] = remote(
            b["seg"].at[0], b["seg"].at[far], b["sg_ss"].at[far - 1], b["sg_rs"].at[far - 1], seq=lax.rem(s + S - t, S)
        )
        go(after[t], s + t < S)
        go(before[t], s - t >= 0)

    r_copies = {}

    waited = set()

    def pack(a, c):
        if a not in waited:
            waited.add(a)
            loads[(1, 2, 5)[a]].wait()
        at = first[c] * HS
        packed = mm(b["sel"][...], b["x"][a, :, at : at + wide[c]], 1, 0).astype(BF16)
        b["snd"][a, c, :, :, : wide[c]] = packed.reshape(D, CP, wide[c])
        b["arr"][a, c, d, :, : wide[c]] = b["snd"][a, c, d, :, : wide[c]]

    def send(a, c):
        for t in range(1, D):
            to = lax.rem(d + t, D)
            copy = remote(
                b["snd"].at[a, c, to, pl.ds(0, CAP), pl.ds(0, wide[c])],
                b["arr"].at[a, c, d, pl.ds(0, CAP), pl.ds(0, wide[c])],
                b["r_ss"].at[a, c, t],
                b["r_rs"].at[a, c, t],
                dp=to,
            )
            go(copy)
            r_copies[a, c, t] = copy

    def masks():
        for t in range(1, S):
            pl.when(s - t >= 0)(after[t].wait_recv)
            pl.when(s + t < S)(before[t].wait_recv)
        across = jnp.broadcast_to(b["seg"][0][0:1, :], (R, R))
        down = jnp.transpose(across)
        t_at = lax.broadcasted_iota(jnp.int32, (R, R), 0)
        u_at = lax.broadcasted_iota(jnp.int32, (R, R), 1)
        b["doc"][...] = jnp.where((u_at <= t_at) & (across == down), 1.0, 0.0)
        own_last = b["seg"][0][0:1, R - 1 : R]
        own_first = b["seg"][0][0:1, 0:1]
        last_before = b["seg"][1][0:1, R - 1 : R]
        first_after = b["seg"][2][0:1, 0:1]
        for i, value in ((TAIL, own_last), (HEAD, own_first), (CAR, last_before), (REV, first_after)):
            b["mk"][i] = jnp.where(down == jnp.broadcast_to(value, (R, R)), 1.0, 0.0).astype(BF16)
        for t in range(1, S):
            last_then = b["seg"][2 * t - 1][0:1, R - 1 : R]
            first_then = b["seg"][2 * t][0:1, 0:1]
            b["jn"][2 * t - 2] = jnp.broadcast_to(jnp.where(last_then == last_before, 1.0, 0.0), (8, R))
            b["jn"][2 * t - 1] = jnp.broadcast_to(jnp.where(first_then == first_after, 1.0, 0.0), (8, R))

    px, off = m // PX, pl.multiple_of((m % PX) * RP, RP)
    g_copies = []

    def turn():
        for c in y_copies:
            c.wait_recv()
        for i in range(M):
            for j in range(DM // HS):
                b["gt"][pl.ds(i * DM + j * HS, HS), :] = jnp.transpose(b["g"][i, :, j * HS : (j + 1) * HS])

    def terms():
        for t in range(D):
            for cc in range(2):
                to, core = lax.rem(d + t, D), (co + cc) % 2
                at = pl.multiple_of(((to * X + px) * 2 + core) * RB + off, RP)
                if t == 0 and cc == 0:
                    b["gz"][d, co, px, pl.ds(off, RP), :] = b["gt"][pl.ds(at, RP), :]
                    continue
                copy = remote(
                    b["gt"].at[pl.ds(at, RP), :],
                    b["gz"].at[d, co, px, pl.ds(off, RP), :],
                    b["g_ss"].at[t * 2 + cc],
                    b["g_rs"].at[t * 2 + cc],
                    dp=to,
                    seq=xi * 2 + core,
                )
                go(copy)
                g_copies.append(copy)

    def grow(c):
        w_loads[c].wait()
        total = mm(b["g"][0], b["w"][c, : wide[c], 0:DM], 1, 1)
        for i in range(1, M):
            total = total + mm(b["g"][i], b["w"][c, : wide[c], i * DM : (i + 1) * DM], 1, 1)
        b["dn"][c, :, : wide[c]] = total

    def place(a, c):
        for t in range(1, D):
            r_copies[a, c, t].wait_recv()
        parts = b["arr"][a, c, :, :, : wide[c]].reshape(D * CP, wide[c])
        b["f"][a, c, :, : wide[c]] = mm(b["pick"][...], parts, 1, 0).astype(BF16)

    s_copies, v_copies = {}, {}

    def part(ref, c, *at):
        return ref.at[(c, *at, slice(None), pl.ds(0, wide[c]))]

    def keep(c):
        place(K, c)
        place(V, c)
        for h in range(HEADS[c]):
            cols = slice(h * HS, (h + 1) * HS)
            term = mm(b["f"][K, c, :, cols] * b["mk"][TAIL], b["f"][V, c, :, cols], 0, 0)
            b["ls"][c, :, cols] = term.astype(BF16)
        for t in range(1, S):
            copy = remote(
                part(b["ls"], c), part(b["sr"], c, t - 1), b["f_ss"].at[c, t - 1], b["f_rs"].at[c, t - 1], seq=lax.rem(s + t, S)
            )
            go(copy, s + t < S)
            s_copies[c, t] = copy

    def gather(c, copies, there, came, kept, side):
        for t in range(1, S):
            pl.when(there(t))(copies[c, t].wait_recv)
        b["tot"][...] = jnp.zeros_like(b["tot"])
        for t in range(1, S):

            @pl.when(there(t))
            def _(t=t):
                run = jnp.broadcast_to(b["jn"][2 * t - 2 + side][0:1, 0:1], (HS, wide[c]))
                b["tot"][:, : wide[c]] += came[c, t - 1, :, : wide[c]].astype(F32) * run

        kept[c] = b["tot"][...].astype(BF16)

    def earlier(c):
        gather(c, s_copies, lambda t: s - t >= 0, b["sr"], b["st"], 0)

    def later(c):
        gather(c, v_copies, lambda t: s + t < S, b["rr"], b["rst"], 1)

    def spread(c, origin, right, left):
        block = part(b["nb"], c, origin, co)
        if right is not None:
            go(remote(block, block, b["nr_ss"].at[c, origin], b["n_rs"].at[c, origin], dp=jnp.minimum(d + 1, D - 1)), right)
        if left is not None:
            go(remote(block, block, b["nl_ss"].at[c, origin], b["n_rs"].at[c, origin], dp=jnp.maximum(d - 1, 0)), left)

    def share(c, origin, cond):
        block = part(b["nb"], c, origin, co)
        go(remote(block, block, b["p_ss"].at[c, origin], b["p_rs"].at[c, origin], seq=xi * 2 + 1 - co), cond)

    loads[6].wait()

    def forward(c):
        place(Q, c)
        earlier(c)
        for h in range(HEADS[c]):
            cols = slice(h * HS, (h + 1) * HS)
            q, k, v = (b["f"][a, c, :, cols] for a in (Q, K, V))
            p = (mm(q, k, 1, 1) * b["doc"][...]).astype(BF16)
            b["pm"][c, :, cols] = p
            both = jnp.concatenate([p, q * b["mk"][CAR]], axis=1)
            attn = mm(both, jnp.concatenate([v, b["st"][c, :, cols]], axis=0), 1, 0)
            gain_h = gain[:, (first[c] + h) * HS : (first[c] + h + 1) * HS]
            scale = lax.rsqrt(jnp.mean(attn * attn, axis=-1, keepdims=True) + NORM_EPS)
            unit = attn * scale
            out = (unit * gain_h).astype(BF16)
            b["nb"][c, d, co, :, cols] = out
            normed_out[c, :, cols] = out
            g = b["dn"][c, :, cols] * gain_h
            d_attn = scale * (g - unit * jnp.mean(g * unit, axis=-1, keepdims=True))
            b["dh"][c, :, cols] = d_attn.astype(BF16)
        spread(c, d, d < D - 1, d > 0)
        share(c, d, None)
        for h in range(HEADS[c]):
            cols = slice(h * HS, (h + 1) * HS)
            term = mm(b["f"][Q, c, :, cols] * b["mk"][HEAD], b["dh"][c, :, cols], 0, 0)
            b["lr"][c, :, cols] = term.astype(BF16)
        for t in range(1, S):
            copy = remote(
                part(b["lr"], c), part(b["rr"], c, t - 1), b["v_ss"].at[c, t - 1], b["v_rs"].at[c, t - 1], seq=lax.rem(s + S - t, S)
            )
            go(copy, s - t >= 0)
            v_copies[c, t] = copy

    def arrived(c, origin):
        block = part(b["nb"], c, origin, co)
        remote(block, block, b["nr_ss"].at[c, origin], b["n_rs"].at[c, origin], dp=lax.rem(d + 1, D)).wait_recv()

    def relay(c, step):
        @pl.when(d - step >= 0)
        def _():
            arrived(c, d - step)

        spread(c, jnp.maximum(d - step, 0), (d - step >= 0) & (d < D - 1), None)
        share(c, jnp.maximum(d - step, 0), d - step >= 0)

        @pl.when(d + step < D)
        def _():
            arrived(c, d + step)

        spread(c, jnp.minimum(d + step, D - 1), None, (d + step < D) & (d > 0))
        share(c, jnp.minimum(d + step, D - 1), d + step < D)

    def backward(c):
        later(c)
        for h in range(HEADS[c]):
            cols = slice(h * HS, (h + 1) * HS)
            q, k, v = (b["f"][a, c, :, cols] for a in (Q, K, V))
            dh, p = b["dh"][c, :, cols], b["pm"][c, :, cols]
            st, rst = b["st"][c, :, cols], b["rst"][c, :, cols]
            dp = (mm(dh, v, 1, 1) * b["doc"][...]).astype(BF16)
            rev = b["mk"][REV]
            grads_out[0, c, :, cols] = (mm(dp, k, 1, 0) + mm(dh * b["mk"][CAR], st, 1, 1)).astype(BF16)
            grads_out[1, c, :, cols] = (mm(dp, q, 0, 0) + mm(v * rev, rst, 1, 1)).astype(BF16)
            grads_out[2, c, :, cols] = (mm(p, dh, 0, 0) + mm(k * rev, rst, 1, 0)).astype(BF16)

    def add(c, origin, t, cols, fresh=False):
        to = lax.rem(xi + t, X)
        left = jnp.concatenate([b["gz"][origin, 0, to], b["gz"][origin, 1, to]], axis=1)
        right = b["nb"][c, origin, :, :, cols].reshape(2 * R, cols.stop - cols.start)
        term = mm(left, right, 1, 0)
        b["acc"][c, t, :, cols] = term if fresh else b["acc"][c, t, :, cols] + term

    def pieces(c):
        half = wide[c] // 2
        return (slice(0, half), slice(half, wide[c])) if wide[c] > 2 * HS and half % HS == 0 else (slice(0, wide[c]),)

    def paired(c, origin):
        block = part(b["nb"], c, origin, 1 - co)
        remote(block, block, b["p_ss"].at[c, origin], b["p_rs"].at[c, origin], seq=xi * 2 + 1 - co).wait_recv()

    def each(step, act):
        if step == 0:
            act(d)
            return
        pl.when(d - step >= 0)(lambda: act(d - step))
        pl.when(d + step < D)(lambda: act(d + step))

    def absorb(c, step):
        def one(origin):
            paired(c, origin)
            for t in range(X):
                add(c, origin, t, slice(0, wide[c]), fresh=step == 0)

        each(step, one)

    x_copies = {}

    def close(c, step):
        each(step, lambda origin: paired(c, origin))
        for t in list(range(1, X)) + [0]:
            for i, cols in enumerate(pieces(c)):
                each(step, lambda origin: add(c, origin, t, cols, fresh=step == 0))
                if t == 0:
                    continue
                b["xs"][c, t - 1, :, cols] = b["acc"][c, t, :, cols].astype(BF16)
                some = pl.ds(cols.start, cols.stop - cols.start)
                copy = remote(
                    b["xs"].at[c, t - 1, :, some],
                    b["xr"].at[c, t - 1, :, some],
                    b["x_ss"].at[c, t - 1, i],
                    b["x_rs"].at[c, t - 1, i],
                    seq=lax.rem(xi + t, X) * 2 + co,
                )
                go(copy)
                x_copies[c, t, i] = copy

    def settle(c):
        for i, cols in enumerate(pieces(c)):
            total = b["acc"][c, 0, :, cols]
            for t in range(1, X):
                x_copies[c, t, i].wait_recv()
                total = total + b["xr"][c, t - 1, :, cols].astype(F32)
            wg_out[c, :, cols] = total

    b_copies = []

    def double():
        for copy in g_copies:
            copy.wait_recv()
        mine = b["gz"].at[:, :, px, pl.ds(off, RP), :]
        for t in range(1, M):
            copy = remote(mine, mine, b["b_ss"].at[t - 1], b["b_rs"].at[t - 1], mp=lax.rem(m + t, M))
            go(copy)
            b_copies.append(copy)

    def doubled():
        for copy in b_copies:
            copy.wait_recv()

    last = D - 1
    acts = dict(
        pack=pack,
        send=send,
        fetch=fetch,
        masks=masks,
        turn=turn,
        terms=terms,
        grow=grow,
        keep=keep,
        forward=forward,
        relay=relay,
        backward=backward,
        double=double,
        doubled=doubled,
        absorb=absorb,
        close=lambda c: close(c, last),
        settle=settle,
    )
    for name, *args in order(NC, D):
        acts[name](*args)
    for cond, copy in sent:
        when(cond, copy.wait_send)


def write_body(heads, normed, grads, wg, *refs):
    outs, sem = refs[:5], refs[5]
    copies = []
    for c, count in enumerate(heads):
        cols, some = pl.ds(sum(heads[:c]) * HS, count * HS), pl.ds(0, count * HS)
        parts = (normed.at[c], grads.at[0, c], grads.at[1, c], grads.at[2, c], wg.at[c])
        for i, (part, out) in enumerate(zip(parts, outs)):
            copies.append(pltpu.make_async_copy(part.at[:, some], out.at[:, cols], sem.at[c, i]))
    for copy in copies:
        copy.start()
    for copy in copies:
        copy.wait()


def solution(mesh):
    def local(queries, key_rows, value_rows, row_plan, segments, norm_gain, out_weight, out_grad):
        rows, width = queries.shape
        z = plan_sizes(mesh, rows, width, out_grad.shape[1])
        scratch = scratch_of(z)
        chunks, span = z["NC"], z["CW"]
        anywhere = pl.BlockSpec(memory_space=pl.ANY)
        vmem = pl.BlockSpec(memory_space=pltpu.VMEM)
        operands = (
            row_plan,
            segments,
            norm_gain.reshape(1, width),
            queries,
            key_rows,
            value_rows,
            out_weight,
            out_grad,
        )
        kept = pl.pallas_call(
            functools.partial(whole_body, z, tuple(scratch)),
            out_shape=[
                pltpu.VMEM((chunks, rows, span), BF16),
                pltpu.VMEM((3, chunks, rows, span), BF16),
                pltpu.VMEM((chunks, z["RB"], span), F32),
            ],
            in_specs=[pl.BlockSpec(memory_space=pltpu.HBM)] * 8,
            out_specs=[vmem] * 3,
            scratch_shapes=list(scratch.values()),
            compiler_params=pltpu.CompilerParams(
                collective_id=0, has_side_effects=True, vmem_limit_bytes=50 * 1024 * 1024
            ),
        )(*(pltpu.with_memory_space_constraint(a, pltpu.HBM) for a in operands))
        half = jax.ShapeDtypeStruct((rows, width), BF16)
        return pl.pallas_call(
            functools.partial(write_body, z["HEADS"]),
            out_shape=[half, half, half, half, jax.ShapeDtypeStruct((z["RB"], width), F32)],
            in_specs=[anywhere] * 3,
            out_specs=[anywhere] * 5,
            scratch_shapes=[pltpu.SemaphoreType.DMA((chunks, 5))],
            compiler_params=pltpu.CompilerParams(vmem_limit_bytes=4 * 1024 * 1024),
        )(*kept)

    placed = (
        P(("dp", "seq"), "mp"),
        P(("dp", "seq"), "mp"),
        P(("dp", "seq"), "mp"),
        P(),
        P("dp", "seq"),
        P("mp"),
        P("mp", None),
        P(("dp", "seq"), "mp"),
    )
    return jax.shard_map(
        local, mesh=mesh, in_specs=placed, out_specs=(P(("dp", "seq"), "mp"),) * 5, check_vma=False
    )
```

time: 107 us -> 100 us (0.935)
  Pallas kernels: 106 us -> 99.5 us
    pallas_call x1, Pallas kernels: 104 us -> 97.5 us  [local(): pl.pallas_call(functools.partial(whole_body, z, tuple(scratch)), out_shap...]
where the time goes in v3:
time: 100 us
  Pallas kernels  99.5 us (100%)
    pallas_call x1, Pallas kernels, local(): pl.pallas_call(functools.partial(whole_body, z, tuple(scratch)), out_shap...  97.5 us

profile of v3, /device:TPU:0, one launch (start us, length us, event | category | flops | bytes accessed | tf_op | source)
XLA Modules:
  0.0 100.3 jit_solution(14896656236873803910)
XLA Ops:
  0.6 97.5 %shard_map.119 = (bf16[4,128,512]{2,1,0:T(8,128)(2,1)S(1)}, bf16[3,4,128,512]{3,2,1,0:T(8,128)(2,1)S(1)}, f32[4,192,512]{2,1,0:T(8,128)S(1)}) custom-call(s32[4,4]{1,0:T(4,128)} %refs_0_.1, s32[1,128]{1,0:T(1,128)} %refs_1_.1, f32[1,2048]{1,0:T(1,128)} %bitcast.1, bf16[128,2048]{1,0:T(8,128)(2,1)} %refs_3_.1, bf16[128,2048]{1,0:T(8,128)(2,1)} %refs_4_.1, ...), custom_call_target="tpu_custom_call" | custom-call | tf_op jit(solution)/shard_map/pallas_call | solution.py:663
  98.1 2.0 %shard_map.120 = (bf16[128,2048]{1,0:T(8,128)(2,1)}, bf16[128,2048]{1,0:T(8,128)(2,1)}, bf16[128,2048]{1,0:T(8,128)(2,1)}, bf16[128,2048]{1,0:T(8,128)(2,1)}, f32[192,2048]{1,0:T(8,128)}) custom-call(bf16[4,128,512]{2,1,0:T(8,128)(2,1)S(1)} %get-tuple-element.8.normed, bf16[3,4,128,512]{3,2,1,0:T(8,128)(2,1)S(1)} %get-tuple-element.9.grads, ...), custom_call_target="tpu_custom_call" | custom-call | tf_op jit(solution)/shard_map/pallas_call | solution.py:678

commit v4 on v3

--- a/solution.py
+++ b/solution.py
@@ -78,7 +78,8 @@
         jn=vm((2 * SO, 8, R), F32),
         sel=vm((D * z["CP"], R), BF16),
         pick=vm((R, D * z["CP"]), BF16),
-        in_s=dma((7,)),
+        in_s=dma((4,)),
+        h_s=dma((3, NC)),
         w_s=dma((NC,)),
         y_ss=dma((max(1, M - 1),)),
         y_rs=dma((max(1, M - 1),)),
@@ -146,7 +147,7 @@
         rows("send", c + 2, Q)
         if c + 2 < n:
             do("grow", c + 2)
-        if 1 <= c < n - 1 and last:
+        if 1 <= c < n - 1 and last > 1:
             do("relay", c - 1, 1)
             left.remove((STEP + c - 1, c - 1, 1))
             early.append((c - 1, 0))
@@ -167,8 +168,6 @@
             due.remove(item)
         do("close", c)
         closed.append(c)
-        if len(closed) > 1:
-            do("settle", closed[-2])
 
     for _, c, k in sorted(left):
         if (c, k) == (n - 1, last):
@@ -199,8 +198,8 @@
             finish(c)
     while behind:
         do("backward", behind.pop(0))
-    if closed:
-        do("settle", closed[-1])
+    for c in closed:
+        do("settle", c)
     return steps
 
 
@@ -238,18 +237,21 @@
     def greet(**where):
         pl.semaphore_signal(barrier, inc=1, device_id=where, device_id_type=MESH)
 
-    sources = (
-        (plan_in, plan),
-        (k_in, b["x"].at[K]),
-        (v_in, b["x"].at[V]),
-        (g_in, b["g"].at[m]),
-        (seg_in, b["segi"]),
-        (q_in, b["x"].at[Q]),
-        (gain_in, gain),
-    )
+    sources = ((plan_in, plan), (g_in, b["g"].at[m]), (seg_in, b["segi"]), (gain_in, gain))
     loads = [pltpu.make_async_copy(a, c, b["in_s"].at[i]) for i, (a, c) in enumerate(sources)]
-    for load in loads:
+    h_loads = {}
+    for c in range(NC):
+        cols = pl.ds(first[c] * HS, wide[c])
+        for a, whole in ((K, k_in), (V, v_in), (Q, q_in)):
+            h_loads[a, c] = pltpu.make_async_copy(whole.at[:, cols], b["x"].at[a, :, cols], b["h_s"].at[a, c])
+    loads[0].start()
+    h_loads[K, 0].start()
+    h_loads[V, 0].start()
+    for load in loads[1:]:
         load.start()
+    for at, load in h_loads.items():
+        if at not in ((K, 0), (V, 0)):
+            load.start()
     w_loads = [
         pltpu.make_async_copy(
             w_in.at[pl.ds(first[c] * HS, wide[c]), :], b["w"].at[c, pl.ds(0, wide[c])], b["w_s"].at[c]
@@ -303,7 +305,7 @@
 
     pl.semaphore_wait(barrier, peers)
 
-    loads[3].wait()
+    loads[1].wait()
     y_copies = []
     for t in range(1, M):
         c = remote(
@@ -311,7 +313,7 @@
         )
         go(c)
         y_copies.append(c)
-    loads[4].wait()
+    loads[2].wait()
     b["seg"][0] = jnp.broadcast_to(b["segi"][...].astype(F32), (8, R))
     after, before = {}, {}
     for t in range(1, S):
@@ -327,12 +329,8 @@
 
     r_copies = {}
 
-    waited = set()
-
     def pack(a, c):
-        if a not in waited:
-            waited.add(a)
-            loads[(1, 2, 5)[a]].wait()
+        h_loads[a, c].wait()
         at = first[c] * HS
         packed = mm(b["sel"][...], b["x"][a, :, at : at + wide[c]], 1, 0).astype(BF16)
         b["snd"][a, c, :, :, : wide[c]] = packed.reshape(D, CP, wide[c])
@@ -463,11 +461,12 @@
         block = part(b["nb"], c, origin, co)
         go(remote(block, block, b["p_ss"].at[c, origin], b["p_rs"].at[c, origin], seq=xi * 2 + 1 - co), cond)
 
-    loads[6].wait()
+    loads[3].wait()
 
     def forward(c):
         place(Q, c)
         earlier(c)
+        held = []
         for h in range(HEADS[c]):
             cols = slice(h * HS, (h + 1) * HS)
             q, k, v = (b["f"][a, c, :, cols] for a in (Q, K, V))
@@ -481,11 +480,15 @@
             out = (unit * gain_h).astype(BF16)
             b["nb"][c, d, co, :, cols] = out
             normed_out[c, :, cols] = out
+            held.append((gain_h, scale, unit))
+        spread(c, d, d < D - 1, d > 0)
+        share(c, d, None)
+        for h in range(HEADS[c]):
+            cols = slice(h * HS, (h + 1) * HS)
+            gain_h, scale, unit = held[h]
             g = b["dn"][c, :, cols] * gain_h
             d_attn = scale * (g - unit * jnp.mean(g * unit, axis=-1, keepdims=True))
             b["dh"][c, :, cols] = d_attn.astype(BF16)
-        spread(c, d, d < D - 1, d > 0)
-        share(c, d, None)
         for h in range(HEADS[c]):
             cols = slice(h * HS, (h + 1) * HS)
             term = mm(b["f"][Q, c, :, cols] * b["mk"][HEAD], b["dh"][c, :, cols], 0, 0)
@@ -501,20 +504,35 @@
         block = part(b["nb"], c, origin, co)
         remote(block, block, b["nr_ss"].at[c, origin], b["n_rs"].at[c, origin], dp=lax.rem(d + 1, D)).wait_recv()
 
+    def from_left(c, step, cond):
+        cond = cond & (d - step >= 0)
+        origin = jnp.maximum(d - step, 0)
+        pl.when(cond)(lambda: arrived(c, d - step))
+        spread(c, origin, cond & (d < D - 1), None)
+        share(c, origin, cond)
+
+    def from_right(c, step, cond):
+        cond = cond & (d + step < D)
+        origin = jnp.minimum(d + step, D - 1)
+        pl.when(cond)(lambda: arrived(c, d + step))
+        spread(c, origin, None, cond & (d > 0))
+        share(c, origin, cond)
+
+    low = d < D // 2
+    high = d >= D // 2
+
+    def inward(c, step):
+        from_left(c, step, low)
+        from_right(c, step, high)
+
+    def outward(c, step):
+        from_right(c, step, low)
+        from_left(c, step, high)
+
     def relay(c, step):
-        @pl.when(d - step >= 0)
-        def _():
-            arrived(c, d - step)
-
-        spread(c, jnp.maximum(d - step, 0), (d - step >= 0) & (d < D - 1), None)
-        share(c, jnp.maximum(d - step, 0), d - step >= 0)
-
-        @pl.when(d + step < D)
-        def _():
-            arrived(c, d + step)
-
-        spread(c, jnp.minimum(d + step, D - 1), None, (d + step < D) & (d > 0))
-        share(c, jnp.minimum(d + step, D - 1), d + step < D)
+        if step < (D + 1) // 2:
+            inward(c, step)
+        outward(c, step)
 
     def backward(c):
         later(c)

time: 100 us -> 101 us (1.010)
  no operation moved by 1% of the time
where the time goes in v4:
time: 101 us
  Pallas kernels  99.7 us (99%)
    pallas_call x1, Pallas kernels, local(): pl.pallas_call(functools.partial(whole_body, z, tuple(scratch)), out_shap...  97.7 us

profile of v4, /device:TPU:0, one launch (start us, length us, event | category | flops | bytes accessed | tf_op | source)
XLA Modules:
  0.0 100.5 jit_solution(6102489719016160167)
XLA Ops:
  0.6 97.7 %shard_map.119 = (bf16[4,128,512]{2,1,0:T(8,128)(2,1)S(1)}, bf16[3,4,128,512]{3,2,1,0:T(8,128)(2,1)S(1)}, f32[4,192,512]{2,1,0:T(8,128)S(1)}) custom-call(s32[4,4]{1,0:T(4,128)} %refs_0_.1, s32[1,128]{1,0:T(1,128)} %refs_1_.1, f32[1,2048]{1,0:T(1,128)} %bitcast.1, bf16[128,2048]{1,0:T(8,128)(2,1)} %refs_3_.1, bf16[128,2048]{1,0:T(8,128)(2,1)} %refs_4_.1, ...), custom_call_target="tpu_custom_call" | custom-call | tf_op jit(solution)/shard_map/pallas_call | solution.py:681
  98.3 2.0 %shard_map.120 = (bf16[128,2048]{1,0:T(8,128)(2,1)}, bf16[128,2048]{1,0:T(8,128)(2,1)}, bf16[128,2048]{1,0:T(8,128)(2,1)}, bf16[128,2048]{1,0:T(8,128)(2,1)}, f32[192,2048]{1,0:T(8,128)}) custom-call(bf16[4,128,512]{2,1,0:T(8,128)(2,1)S(1)} %get-tuple-element.8.normed, bf16[3,4,128,512]{3,2,1,0:T(8,128)(2,1)S(1)} %get-tuple-element.9.grads, ...), custom_call_target="tpu_custom_call" | custom-call | tf_op jit(solution)/shard_map/pallas_call | solution.py:696
